TPU v7x, 32 devices: a whole 2x2x4 slice. The times are simulated.
32 devices in a mesh: dp: 16 (over z, y, core), tensor: 2 (over x).
Axes of the slice: x: 2, y: 2, z: 4, core: 2. Of those that a mesh axis runs over, the one named last changes fastest.
Arguments:
- tokens: bfloat16 [4096, 1024], P(('dp', 'tensor')), may hold values from -24 to 24, as said below
- segment_ids: int32 [16, 256], P('dp'), may hold values from 0 to 3, never falling along the last dimension, each value on 1 to 128 neighbouring positions
- norm1_gain: float32 [1024], replicated, may hold values from 0.5 to 1.5
- in_proj: bfloat16 [1024, 3, 1024], P('dp', None, 'tensor'), may hold values from -0.1875 to 0.1875
- conv_weight: float32 [3, 1024], replicated, may hold values from -3 to 3
- out_proj: bfloat16 [1024, 1024], P('dp', 'tensor'), may hold values from -0.1875 to 0.1875
- norm2_gain: float32 [1024], replicated, may hold values from 0.5 to 1.5
- gate_up: bfloat16 [1024, 2, 4608], P('dp', None, 'tensor'), may hold values from -0.1875 to 0.1875
- down_proj: bfloat16 [1024, 4608], P('dp', 'tensor'), may hold values from -0.1875 to 0.1875
- cotangent: bfloat16 [4096, 1024], P(('dp', 'tensor')), may hold values from -6 to 6
Outputs:
- block_out: float32 [4096, 1024], P(('dp', 'tensor'))
- grad_tokens: float32 [4096, 1024], P(('dp', 'tensor'))
- grad_norm1: float32 [1024], replicated
- grad_in_proj: float32 [1024, 3, 1024], P('dp', None, 'tensor')
- grad_conv: float32 [3, 1024], replicated
- grad_out_proj: float32 [1024, 1024], P('dp', 'tensor')
- grad_norm2: float32 [1024], replicated
- grad_gate_up: float32 [1024, 2, 4608], P('dp', None, 'tensor')
- grad_down: float32 [1024, 4608], P('dp', 'tensor')
Inputs may be any that keep to these rules, and one draw needn't show every extreme that they name: `segment_ids`: along each row the document numbers never fall; each document spans 1 to 128 tokens and one spans exactly 128. `tokens`: real values.
All inputs are finite; a program needn't handle non-finite values.
Results may differ from a plain program's by a relative error of at most 0.009.
Values may be sent and summed in bfloat16 or wider, within the bound.
A program may use at most 128 MiB of HBM per device.

v0:
```python
import jax
import jax.numpy as jnp
from jax import lax
from jax.sharding import PartitionSpec as P

EPSILON = 1e-05


def rms_forward(values, norm_gain):
    factor = lax.rsqrt(jnp.mean(values * values, axis=-1, keepdims=True) + EPSILON)
    return (values * factor * norm_gain, factor)


def rms_backward(values, factor, norm_gain, upstream):
    scaled = upstream * norm_gain
    result = factor * scaled - values * (factor * factor * factor) * jnp.mean(
        scaled * values, axis=-1, keepdims=True
    )
    return (result, jnp.sum(upstream * values * factor, axis=0))


def lagged(values, offset):
    return jnp.concatenate(
        [jnp.zeros((offset, values.shape[1]), values.dtype), values[:-offset]], axis=0
    )


def leading(values, offset):
    return jnp.concatenate(
        [values[offset:], jnp.zeros((offset, values.shape[1]), values.dtype)], axis=0
    )


def reset_masks(segment):
    same_one = jnp.concatenate([jnp.zeros((1,), jnp.bool_), segment[1:] == segment[:-1]])
    same_two = jnp.concatenate([jnp.zeros((2,), jnp.bool_), segment[2:] == segment[:-2]])
    return (same_one.astype(jnp.float32)[:, None], same_two.astype(jnp.float32)[:, None])


def conv_forward(values, kernel, mask_one, mask_two):
    return (
        kernel[0] * values
        + kernel[1] * mask_one * lagged(values, 1)
        + kernel[2] * mask_two * lagged(values, 2)
    )


def conv_backward(values, upstream, kernel, mask_one, mask_two):
    result = (
        kernel[0] * upstream
        + leading(kernel[1] * mask_one * upstream, 1)
        + leading(kernel[2] * mask_two * upstream, 2)
    )
    grads = jnp.stack(
        [
            jnp.sum(upstream * values, axis=0),
            jnp.sum(upstream * mask_one * lagged(values, 1), axis=0),
            jnp.sum(upstream * mask_two * lagged(values, 2), axis=0),
        ]
    )
    return (result, grads)


def local(
    tokens,
    segment_ids,
    norm1_gain,
    in_proj,
    conv_weight,
    out_proj,
    norm2_gain,
    gate_up,
    down_proj,
    cotangent,
):
    in_full, out_full = (
        lax.all_gather(in_proj, "dp", axis=0, tiled=True),
        lax.all_gather(out_proj, "dp", axis=0, tiled=True),
    )
    lift_full, down_full = (
        lax.all_gather(gate_up, "dp", axis=0, tiled=True),
        lax.all_gather(down_proj, "dp", axis=0, tiled=True),
    )
    channels = in_proj.shape[2]
    offset = lax.axis_index("tensor") * channels
    kernel = lax.dynamic_slice_in_dim(conv_weight, offset, channels, 1)
    mask_one, mask_two = reset_masks(segment_ids[0])
    inputs = tokens.astype(jnp.float32)
    normed_one, factor_one = rms_forward(inputs, norm1_gain)
    rows_one = lax.all_gather(normed_one.astype(jnp.bfloat16), "tensor", axis=0, tiled=True)
    projected = jnp.einsum("td,djc->jtc", rows_one, in_full, preferred_element_type=jnp.float32)
    b_part, c_part, x_part = (projected[0], projected[1], projected[2])
    mixed_in = b_part * x_part
    conv_out = conv_forward(mixed_in, kernel, mask_one, mask_two)
    gated = (c_part * conv_out).astype(jnp.bfloat16)
    mixer_terms = jnp.einsum("tc,dc->td", gated, out_full, preferred_element_type=jnp.float32)
    resid = inputs + lax.psum_scatter(mixer_terms, "tensor", scatter_dimension=0, tiled=True)
    normed_two, factor_two = rms_forward(resid, norm2_gain)
    rows_two = lax.all_gather(normed_two.astype(jnp.bfloat16), "tensor", axis=0, tiled=True)
    lifted = jnp.einsum("td,djf->jtf", rows_two, lift_full, preferred_element_type=jnp.float32)
    gate_lin, up_lin = (lifted[0], lifted[1])
    sigmoid_gate = jax.nn.sigmoid(gate_lin)
    activ = gate_lin * sigmoid_gate
    hidden = (activ * up_lin).astype(jnp.bfloat16)
    ffn_terms = jnp.einsum("tf,df->td", hidden, down_full, preferred_element_type=jnp.float32)
    block_out = resid + lax.psum_scatter(
        ffn_terms.astype(jnp.bfloat16), "tensor", scatter_dimension=0, tiled=True
    ).astype(jnp.float32)
    cot_rows = lax.all_gather(cotangent, "tensor", axis=0, tiled=True)
    grad_down = jnp.einsum("td,tf->df", cot_rows, hidden, preferred_element_type=jnp.float32)
    back_hidden = jnp.einsum("td,df->tf", cot_rows, down_full, preferred_element_type=jnp.float32)
    back_gate = (
        back_hidden * up_lin * sigmoid_gate * (1.0 + gate_lin * (1.0 - sigmoid_gate))
    ).astype(jnp.bfloat16)
    back_up = (back_hidden * activ).astype(jnp.bfloat16)
    back_lifted = jnp.stack([back_gate, back_up])
    grad_lift = jnp.einsum("td,jtf->djf", rows_two, back_lifted, preferred_element_type=jnp.float32)
    normed_terms = jnp.einsum(
        "jtf,djf->td", back_lifted, lift_full, preferred_element_type=jnp.float32
    )
    back_normed2 = lax.psum_scatter(normed_terms, "tensor", scatter_dimension=0, tiled=True)
    resid_part, gain_two = rms_backward(resid, factor_two, norm2_gain, back_normed2)
    back_resid = cotangent.astype(jnp.float32) + resid_part
    resid_rows = lax.all_gather(back_resid.astype(jnp.bfloat16), "tensor", axis=0, tiled=True)
    grad_out = jnp.einsum("td,tc->dc", resid_rows, gated, preferred_element_type=jnp.float32)
    back_gated = jnp.einsum("td,dc->tc", resid_rows, out_full, preferred_element_type=jnp.float32)
    back_c = back_gated * conv_out
    back_conv = back_gated * c_part
    back_mixed, conv_local = conv_backward(mixed_in, back_conv, kernel, mask_one, mask_two)
    back_proj = jnp.stack([back_mixed * x_part, back_c, back_mixed * b_part]).astype(jnp.bfloat16)
    grad_in = jnp.einsum("td,jtc->djc", rows_one, back_proj, preferred_element_type=jnp.float32)
    input_terms = jnp.einsum("jtc,djc->td", back_proj, in_full, preferred_element_type=jnp.float32)
    back_normed1 = lax.psum_scatter(input_terms, "tensor", scatter_dimension=0, tiled=True)
    input_part, gain_one = rms_backward(inputs, factor_one, norm1_gain, back_normed1)
    grad_tokens = back_resid + input_part
    conv_placed = lax.dynamic_update_slice_in_dim(
        jnp.zeros(conv_weight.shape, jnp.float32), conv_local, offset, 1
    )
    gain_one, gain_two, conv_total = lax.psum((gain_one, gain_two, conv_placed), ("dp", "tensor"))
    in_shard, out_shard, lift_shard, down_shard = (
        lax.psum_scatter(grad_in, "dp", scatter_dimension=0, tiled=True),
        lax.psum_scatter(grad_out, "dp", scatter_dimension=0, tiled=True),
        lax.psum_scatter(grad_lift, "dp", scatter_dimension=0, tiled=True),
        lax.psum_scatter(grad_down, "dp", scatter_dimension=0, tiled=True),
    )
    return (
        block_out,
        grad_tokens,
        gain_one,
        in_shard,
        conv_total,
        out_shard,
        gain_two,
        lift_shard,
        down_shard,
    )


def solution(mesh):
    placed = (
        P(("dp", "tensor"), None),
        P("dp", None),
        P(),
        P("dp", None, "tensor"),
        P(),
        P("dp", "tensor"),
        P(),
        P("dp", None, "tensor"),
        P("dp", "tensor"),
        P(("dp", "tensor"), None),
    )
    return jax.shard_map(
        local,
        mesh=mesh,
        in_specs=placed,
        out_specs=(
            P(("dp", "tensor"), None),
            P(("dp", "tensor"), None),
            P(),
            P("dp", None, "tensor"),
            P(),
            P("dp", "tensor"),
            P(),
            P("dp", None, "tensor"),
            P("dp", "tensor"),
        ),
        check_vma=False,
    )
```

profile of v0, /device:TPU:0, one launch (start us, length us, event | category | flops | bytes accessed | tf_op | source)
XLA Modules:
  0.0 817.8 jit_solution(3334355280649713544)
XLA Ops:
  7.2 0.7 all-gather.5.cloned.1.call-update
  8.0 0.7 all-gather.7.cloned.1.call-update
  8.7 0.8 compare_reduce_fusion.1
  9.6 0.8 compare_reduce_fusion
  10.4 0.1 add_convert_fusion
  10.5 0.9 constant_dynamic-slice_fusion
  11.4 1.1 fusion.6
  12.5 1.1 fusion.8
  13.6 9.9 %all_gather.24 = bf16[256,1024]{1,0:T(8,128)(2,1)S(1)} all-gather(bf16[128,1024]{1,0:T(8,128)(2,1)S(1)} %fusion.8), channel_id=1, replica_groups=mesh['dp'=16,'tensor'=2] {'tensor'}, dimensions={0}, use_global_device_ids=true | all-gather | bytes 786432 | tf_op jit(solution)/shard_map/all_gather | solution.py:90
  23.5 34.8 %all-gather.5.cloned.1.call-done = bf16[1024,3,512]{2,0,1:T(8,128)(2,1)} async-done(((bf16[64,3,512]{2,0,1:T(8,128)(2,1)}), bf16[1024,3,512]{2,0,1:T(8,128)(2,1)}) %all-gather.5.cloned.1.call-update) | async-done | bytes 3145744 | tf_op jit(solution)/shard_map/all_gather | solution.py:77
  58.3 2.9 convolution_bitcast_fusion.2
  61.1 0.1 fusion.21
  61.2 1.4 multiply_convert_fusion.7
  62.6 34.1 %all-gather.7.cloned.1.call-done = bf16[1024,512]{1,0:T(8,128)(2,1)} async-done(((bf16[64,512]{1,0:T(8,128)(2,1)}), bf16[1024,512]{1,0:T(8,128)(2,1)}) %all-gather.7.cloned.1.call-update) | async-done | bytes 1048592 | tf_op jit(solution)/shard_map/all_gather | solution.py:78
  96.7 2.7 fusion.31
  99.5 0.9 copy.24
  100.4 0.5 all-gather.11.cloned.1.call-update
  101.0 13.6 %all_gather.30 = bf16[256,1024]{1,0:T(8,128)(2,1)} all-gather(bf16[128,1024]{1,0:T(8,128)(2,1)S(1)} %copy-done.16), channel_id=1, replica_groups=mesh['dp'=16,'tensor'=2] {'tensor'}, dimensions={0}, use_global_device_ids=true | all-gather | bytes 786432 | tf_op jit(solution)/shard_map/all_gather | solution.py:109
  114.7 7.9 reduce-scatter.11.cloned.1.call-done
  122.6 1.2 multiply_reduce_fusion.5
  123.8 0.1 multiply_convert_fusion.6
  123.9 8.8 %all_gather.27 = bf16[256,1024]{1,0:T(8,128)(2,1)S(1)} all-gather(bf16[128,1024]{1,0:T(8,128)(2,1)S(1)} %multiply_convert_fusion.6), channel_id=1, replica_groups=mesh['dp'=16,'tensor'=2] {'tensor'}, dimensions={0}, use_global_device_ids=true | all-gather | bytes 786432 | tf_op jit(solution)/shard_map/all_gather | solution.py:99
  132.8 72.5 %all-gather.9.cloned.1.call-done = bf16[1024,2,2304]{2,0,1:T(8,128)(2,1)} async-done(((bf16[64,2,2304]{2,0,1:T(8,128)(2,1)}), bf16[1024,2,2304]{2,0,1:T(8,128)(2,1)}) %all-gather.9.cloned.1.call-update) | async-done | bytes 9437200 | tf_op jit(solution)/shard_map/all_gather | solution.py:81
  205.2 8.0 convolution_bitcast_fusion.1
  213.2 45.7 %all-gather.11.cloned.1.call-done = bf16[1024,2304]{1,0:T(8,128)(2,1)} async-done(((bf16[64,2304]{1,0:T(8,128)(2,1)}), bf16[1024,2304]{1,0:T(8,128)(2,1)}) %all-gather.11.cloned.1.call-update) | async-done | bytes 4718608 | tf_op jit(solution)/shard_map/all_gather | solution.py:82
  258.9 6.9 fusion.5
  265.9 1.0 copy-done.13
  266.9 0.4 copy-done.15
  267.3 3.6 fusion.3
  271.0 4.9 convolution_convert_fusion
  276.0 14.1 %reduce-scatter.15.cloned.1.call-done = f32[128,1024]{1,0:T(8,128)} async-done(((f32[256,1024]{1,0:T(8,128)}), f32[128,1024]{1,0:T(8,128)}) %reduce-scatter.15.cloned.1.call-update) | async-done | bytes 524304 | tf_op jit(solution)/shard_map/reduce_scatter | solution.py:121
  290.1 1.2 multiply_reduce_fusion
  291.3 16.2 %reduce-scatter.13.cloned.1.call-done = bf16[128,1024]{1,0:T(8,128)(2,1)} async-done(((bf16[256,1024]{1,0:T(8,128)(2,1)}), bf16[128,1024]{1,0:T(8,128)(2,1)}) %reduce-scatter.13.cloned.1.call-update) | async-done | bytes 262160 | tf_op jit(solution)/shard_map/reduce_scatter | solution.py:106
  307.5 2.5 fusion.30
  310.0 8.6 %all_gather.31 = bf16[256,1024]{1,0:T(8,128)(2,1)S(1)} all-gather(bf16[128,1024]{1,0:T(8,128)(2,1)S(1)} %get-tuple-element.40), channel_id=1, replica_groups=mesh['dp'=16,'tensor'=2] {'tensor'}, dimensions={0}, use_global_device_ids=true | all-gather | bytes 786432 | tf_op jit(solution)/shard_map/all_gather | solution.py:124
  318.6 0.6 multiply_reduce_fusion.3
  319.2 0.4 copy-done.6
  319.6 0.1 slice_multiply_fusion
  319.7 0.0 copy-done.5
  319.8 0.1 slice_multiply_fusion.1
  319.9 0.2 fusion.22
  320.2 0.1 fusion.24
  320.3 0.6 copy-done.19
  320.9 1.0 copy-done.24
  321.9 2.0 convolution_bitcast_fusion.3
  323.9 0.2 reduce-scatter.23.cloned.1.call-start
  324.1 9.4 %fusion.1 = f32[1024,2,2304]{2,0,1:T(8,128)} fusion(bf16[1,256,2304]{2,1,0:T(8,128)(2,1)} %copy-done.15, bf16[1,256,2304]{2,1,0:T(8,128)(2,1)S(1)} %copy-done.14, bf16[256,1024]{1,0:T(8,128)(2,1)S(1)} %all_gather.27), kind=kOutput, calls=%fused_computation.10 | convolution fusion | flops 2420637696 | bytes 21757952 | tf_op jit(solution)/shard_map/td,jtf->djf/dot_general | solution.py:117
  333.6 0.8 copy-done.4
  334.4 1.8 fusion.32
  336.3 3.7 fusion.17
  340.0 0.0 reduce-scatter.25.cloned.1.call-start
  340.1 1.0 copy-done.10
  341.0 0.4 copy-done.12
  341.4 5.1 convolution_bitcast_fusion
  346.5 10.1 %copy.33 = f32[1024,2304]{1,0:T(8,128)} copy(f32[1024,2304]{0,1:T(8,128)} %convolution_bitcast_fusion) | data formatting | bytes 18874368
  356.7 0.6 copy-done.23
  357.3 1.3 fusion.14
  358.6 40.1 %all-reduce.5 = (f32[1024]{0:T(1024)}, f32[3,1024]{1,0:T(4,128)}, f32[1024]{0:T(1024)}) all-reduce(f32[1024]{0:T(1024)S(1)} %get-tuple-element.29, f32[3,1024]{1,0:T(4,128)S(1)} %maximum_dynamic-update-slice_fusion, f32[1024]{0:T(1024)S(1)} %get-tuple-element.27), channel_id=1, replica_groups=mesh['dp'=16,'tensor'=2] {'dp','tensor'}, use_global_device_ids=true, to_apply=%region_9.0 | all-reduce | flops 5120 | bytes 40960 | tf_op jit(solution)/shard_map/psum | solution.py:139
  398.7 2.1 fusion.11
  400.8 141.7 %reduce-scatter.23.cloned.1.call-done = f32[64,2,2304]{2,0,1:T(8,128)} async-done(((f32[1024,2,2304]{2,0,1:T(8,128)}), f32[64,2,2304]{2,0,1:T(8,128)}) %reduce-scatter.23.cloned.1.call-update) | async-done | bytes 1179664 | tf_op jit(solution)/shard_map/reduce_scatter | solution.py:143
  542.5 3.2 copy.27
  545.7 61.9 %reduce-scatter.21.cloned.1.call-done = f32[64,512]{1,0:T(8,128)} async-done(((f32[1024,512]{1,0:T(8,128)}), f32[64,512]{1,0:T(8,128)}) %reduce-scatter.21.cloned.1.call-update) | async-done | bytes 131088 | tf_op jit(solution)/shard_map/reduce_scatter | solution.py:142
  607.6 88.5 %reduce-scatter.19.cloned.1.call-done = f32[64,3,512]{2,0,1:T(8,128)} async-done(((f32[1024,3,512]{2,0,1:T(8,128)}), f32[64,3,512]{2,0,1:T(8,128)}) %reduce-scatter.19.cloned.1.call-update) | async-done | bytes 393232 | tf_op jit(solution)/shard_map/reduce_scatter | solution.py:141
  696.1 114.9 %reduce-scatter.25.cloned.1.call-done = f32[64,2304]{1,0:T(8,128)} async-done(((f32[1024,2304]{1,0:T(8,128)}), f32[64,2304]{1,0:T(8,128)}) %reduce-scatter.25.cloned.1.call-update) | async-done | bytes 589840
  (66 shorter events, 0.7 us)
Async XLA Ops:
  7.2 51.1 %all-gather.5.cloned.1.call-start = ((), (), s32[]{:S(2)}) async-start(), calls=%async_computation.8 | async-start | bytes 3342336 | tf_op jit(solution)/shard_map/all_gather | solution.py:77
  7.9 88.8 %all-gather.7.cloned.1.call-start = ((), (), s32[]{:S(2)}) async-start(), calls=%async_computation.9 | async-start | bytes 1114112 | tf_op jit(solution)/shard_map/all_gather | solution.py:78
  8.7 113.9 %reduce-scatter.11.cloned.1.call-start = ((), (), s32[]{:S(2)}) async-start(), calls=%async_computation.10 | async-start | bytes 1572864 | tf_op jit(solution)/shard_map/reduce_scatter | solution.py:97
  23.5 34.8 %copy-start.8 = (bf16[256,1024]{1,0:T(8,128)(2,1)}, bf16[256,1024]{1,0:T(8,128)(2,1)S(1)}, u32[]{:S(2)}) copy-start(bf16[256,1024]{1,0:T(8,128)(2,1)S(1)} %all_gather.24) | copy-start | bytes 1572868
  62.6 37.8 %copy-start.3 = (bf16[256,512]{1,0:T(8,128)(2,1)}, bf16[256,512]{1,0:T(8,128)(2,1)S(1)}, u32[]{:S(2)}) copy-start(bf16[256,512]{1,0:T(8,128)(2,1)S(1)} %get-tuple-element.44) | copy-start | bytes 786436
  62.6 36.9 %copy-start.21 = (bf16[64,2,2304]{2,1,0:T(2,128)(2,1)S(1)}, bf16[64,2,2304]{2,1,0:T(2,128)(2,1)}, u32[]{:S(2)}) copy-start(bf16[64,2,2304]{2,1,0:T(2,128)(2,1)} %param.17) | copy-start | bytes 1769476
  96.7 4.3 copy-start.16
  99.4 23.2 %copy-start.1 = (bf16[128,1024]{1,0:T(8,128)(2,1)S(1)}, bf16[128,1024]{1,0:T(8,128)(2,1)}, u32[]{:S(2)}) copy-start(bf16[128,1024]{1,0:T(8,128)(2,1)} %param.10) | copy-start | bytes 786436
  99.4 24.4 %copy-start.22 = (f32[1024]{0:T(1024)S(1)}, f32[1024]{0:T(1024)}, u32[]{:S(2)}) copy-start(f32[1024]{0:T(1024)} %param.16) | copy-start | bytes 12292
  99.4 105.8 %all-gather.9.cloned.1.call-start = ((), (), s32[]{:S(2)}) async-start(), calls=%async_computation.11 | async-start | bytes 10027008 | tf_op jit(solution)/shard_map/all_gather | solution.py:81
  100.4 158.5 %all-gather.11.cloned.1.call-start = ((), (), s32[]{:S(2)}) async-start(), calls=%async_computation.12 | async-start | bytes 5013504 | tf_op jit(solution)/shard_map/all_gather | solution.py:82
  101.0 189.1 %reduce-scatter.15.cloned.1.call-start = ((), (), s32[]{:S(2)}) async-start(), calls=%async_computation.14 | async-start | bytes 1572864 | tf_op jit(solution)/shard_map/reduce_scatter | solution.py:121
  258.9 8.4 %copy-start = (bf16[1024,2,2304]{2,0,1:T(8,128)(2,1)S(1)}, bf16[1024,2,2304]{2,0,1:T(8,128)(2,1)}, u32[]{:S(2)}) copy-start(bf16[1024,2,2304]{2,0,1:T(8,128)(2,1)} %all-gather.9.cloned.1.call-done) | copy-start | bytes 28311556
  265.9 1.0 copy-start.13
  265.9 1.4 copy-start.15
  271.0 36.6 %reduce-scatter.13.cloned.1.call-start = ((), (), s32[]{:S(2)}) async-start(), calls=%async_computation.13 | async-start | bytes 786432 | tf_op jit(solution)/shard_map/reduce_scatter | solution.py:106
  276.0 80.7 %reduce-scatter.17.cloned.1.call-start = ((), (), s32[]{:S(2)}) async-start(), calls=%async_computation.15 | async-start | bytes 1572864 | tf_op jit(solution)/shard_map/reduce_scatter | solution.py:133
  307.5 11.0 %copy-start.2 = (bf16[1024,512]{1,0:T(8,128)(2,1)S(1)}, bf16[1024,512]{1,0:T(8,128)(2,1)}, u32[]{:S(2)}) copy-start(bf16[1024,512]{1,0:T(8,128)(2,1)} %all-gather.7.cloned.1.call-done) | copy-start | bytes 3145732
  307.5 11.0 %copy-start.7 = (f32[256,512]{1,0:T(8,128)S(1)}, f32[256,512]{1,0:T(8,128)}, u32[]{:S(2)}) copy-start(f32[256,512]{1,0:T(8,128)} %get-tuple-element.45) | copy-start | bytes 1572868
  318.6 1.0 copy-start.6
  318.6 1.2 copy-start.5
  319.2 1.0 copy-start.17
  319.9 2.0 copy-start.24
  320.2 0.7 copy-start.19
  321.9 2.2 copy-start.14
  323.9 218.6 %reduce-scatter.23.cloned.1.call-start = ((), (), s32[]{:S(2)}) async-start(), calls=%async_computation.18 | async-start | bytes 20054016 | tf_op jit(solution)/shard_map/reduce_scatter | solution.py:143
  333.5 0.9 copy-start.4
  333.5 2.8 copy-start.9
  333.5 2.8 copy-start.18
  333.5 2.8 copy-start.20
  333.5 274.0 %reduce-scatter.21.cloned.1.call-start = ((), (), s32[]{:S(2)}) async-start(), calls=%async_computation.17 | async-start | bytes 2228224 | tf_op jit(solution)/shard_map/reduce_scatter | solution.py:142
  336.2 359.8 %reduce-scatter.19.cloned.1.call-start = ((), (), s32[]{:S(2)}) async-start(), calls=%async_computation.16 | async-start | bytes 6684672 | tf_op jit(solution)/shard_map/reduce_scatter | solution.py:141
  340.0 1.0 copy-start.10
  340.0 1.4 copy-start.12
  340.0 471.0 %reduce-scatter.25.cloned.1.call-start = ((), (), s32[]{:S(2)}) async-start(), calls=%async_computation.19 | async-start | bytes 10027008
  356.6 0.7 copy-start.23
  356.6 42.1 %copy-start.11 = (f32[128,1024]{1,0:T(8,128)S(1)}, f32[128,1024]{1,0:T(8,128)}, u32[]{:S(2)}) copy-start(f32[128,1024]{1,0:T(8,128)} %get-tuple-element.41) | copy-start | bytes 1572868
Sparse Core Ops, SparseCore 0:
  10.2 48.0 all-gather.4
  60.4 36.2 all-gather.6
  99.5 23.0 reduce-scatter.10
  125.3 79.8 all-gather.8
  207.4 51.5 all-gather.10
  271.1 18.9 reduce-scatter.14
  292.9 14.6 reduce-scatter.12
  324.0 20.3 reduce-scatter.16
  348.5 193.8 reduce-scatter.22
  546.6 60.8 reduce-scatter.20
  612.1 83.9 reduce-scatter.18
  700.6 110.3 reduce-scatter.24
where the time goes:
time: 819 us; the launch traced here: 818 us
  waiting for transfers between devices  634 us (77%)
  blocking collectives  81.1 us (10%)
  matrix products  51.5 us (6%)
  local copies, waits for them, and re-layouts  21.4 us (3%)
  between operations  14.4 us (2%)
  other arithmetic  14.3 us (2%)
    reduce_scatter x1, waiting for transfers between devices, local(): lax.psum_scatter(grad_lift, 'dp', scatter_dimension=0, tiled=True)  142 us
    unnamed x13, waiting for transfers between devices  117 us
    reduce_scatter x1, waiting for transfers between devices, local(): lax.psum_scatter(grad_in, 'dp', scatter_dimension=0, tiled=True)  88.5 us
    all_gather x1, waiting for transfers between devices, local(): lax.all_gather(gate_up, 'dp', axis=0, tiled=True)  72.5 us
    reduce_scatter x1, waiting for transfers between devices, local(): lax.psum_scatter(grad_out, 'dp', scatter_dimension=0, tiled=True)  61.9 us
    all_gather x1, waiting for transfers between devices, local(): lax.all_gather(down_proj, 'dp', axis=0, tiled=True)  45.7 us
    psum x1, blocking collectives, local(): lax.psum((gain_one, gain_two, conv_placed), ('dp', 'tensor'))  40.1 us
    all_gather x1, waiting for transfers between devices, local(): lax.all_gather(in_proj, 'dp', axis=0, tiled=True)  34.8 us
  transfers between devices with their start and end apart: 12, of which 11 were waited for; matrix products, arithmetic and copies ran while one was open for 8% of the time, Pallas kernels for 0%

commit v1 on v0

v1 whole, which is shorter than its diff:
```python
import functools

import jax
import jax.numpy as jnp
from jax import lax
from jax.experimental import pallas as pl
from jax.experimental.pallas import tpu as pltpu
from jax.sharding import PartitionSpec as P

EPSILON = 1e-05


def rms_forward(values, norm_gain):
    factor = lax.rsqrt(jnp.mean(values * values, axis=-1, keepdims=True) + EPSILON)
    return (values * factor * norm_gain, factor)


def rms_backward(values, factor, norm_gain, upstream):
    scaled = upstream * norm_gain
    result = factor * scaled - values * (factor * factor * factor) * jnp.mean(
        scaled * values, axis=-1, keepdims=True
    )
    return (result, jnp.sum(upstream * values * factor, axis=0))


MESH = pl.DeviceIdType.MESH


def chip_at(pos, chips):
    back = pos // (chips // 2)
    return (1 - back) * 2 * pos + back * (2 * (chips - 1 - pos) + 1)


def ring_place(chips):
    me = lax.axis_index("dp")
    core, chip = me % 2, me // 2
    odd = chip % 2
    pos = (1 - odd) * (chip // 2) + odd * (chips - 1 - chip // 2)

    def owner(steps):
        return chip_at((pos + steps + 2 * chips) % chips, chips)

    return me, core, chip, owner


def greet(others):
    barrier = pltpu.get_barrier_semaphore()
    for other in others:
        pl.semaphore_signal(barrier, inc=1, device_id={"dp": other}, device_id_type=MESH)
    pl.semaphore_wait(barrier, len(others))


def gather_kernel(chips, ways, *refs):
    count = len(ways)
    ins, outs = refs[:count], refs[count : 2 * count]
    own_sem, send_sem, recv_sem, hand_sem, take_sem = refs[2 * count :]
    me, core, chip, owner = ring_place(chips)
    partner = chip * 2 + 1 - core
    nexts = {way: owner(way) * 2 + core for way in (1, -1)}
    greet((nexts[1], nexts[-1], partner))
    own, started = [], []
    arriving = [None] * count
    for step in range(chips):
        for i, way in enumerate(ways):
            slot = owner(-way * step) * 2 + core
            if step:
                arriving[i].wait_recv()
            source = outs[i].at[slot] if step else ins[i]
            if step < chips - 1:
                ring = pltpu.make_async_remote_copy(
                    src_ref=source,
                    dst_ref=outs[i].at[slot],
                    send_sem=send_sem.at[i, step],
                    recv_sem=recv_sem.at[i, step],
                    device_id={"dp": nexts[way]},
                    device_id_type=MESH,
                )
                ring.start()
                arriving[i] = ring
                started.append((ring, False))
            hand = pltpu.make_async_remote_copy(
                src_ref=source,
                dst_ref=outs[i].at[slot],
                send_sem=hand_sem.at[i, step],
                recv_sem=take_sem.at[i, step],
                device_id={"dp": partner},
                device_id_type=MESH,
            )
            hand.start()
            started.append((hand, True))
            if step == 0:
                keep = pltpu.make_async_copy(ins[i], outs[i].at[me], own_sem.at[i])
                keep.start()
                own.append(keep)
    for copy, handed in started:
        copy.wait_send()
        if handed:
            copy.wait_recv()
    for keep in own:
        keep.wait()


def gather_all(shards, ways, ranks):
    chips, count = ranks // 2, len(shards)
    dma = pltpu.SemaphoreType.DMA
    gathered = pl.pallas_call(
        functools.partial(gather_kernel, chips, ways),
        out_shape=[jax.ShapeDtypeStruct((ranks,) + s.shape, s.dtype) for s in shards],
        in_specs=[pl.BlockSpec(memory_space=pltpu.VMEM)] * count,
        out_specs=[pl.BlockSpec(memory_space=pl.ANY)] * count,
        scratch_shapes=[
            dma((count,)),
            dma((count, chips - 1)),
            dma((count, chips - 1)),
            dma((count, chips)),
            dma((count, chips)),
        ],
        compiler_params=pltpu.CompilerParams(collective_id=1, has_side_effects=True),
    )(*shards)
    return [g.reshape(ranks * s.shape[0], s.shape[1]) for g, s in zip(gathered, shards)]


def scatter_kernel(chips, ways, *refs):
    count = len(ways)
    ins, outs = refs[:count], refs[count : 2 * count]
    mine = refs[2 * count : 3 * count]
    theirs = refs[3 * count : 4 * count]
    moving = refs[4 * count : 5 * count]
    load_sem, send_sem, recv_sem, hand_sem, take_sem = refs[5 * count :]
    me, core, chip, owner = ring_place(chips)
    partner = chip * 2 + 1 - core
    nexts = {way: owner(way) * 2 + core for way in (1, -1)}
    greet((nexts[1], nexts[-1], partner))
    loads, swaps = {}, {}
    for step in range(chips):
        for i, way in enumerate(ways):
            target = owner(-way * (step + 1))
            load = pltpu.make_async_copy(
                ins[i].at[target * 2 + core], mine[i].at[step], load_sem.at[i, step]
            )
            load.start()
            loads[i, step] = load
            swap = pltpu.make_async_remote_copy(
                src_ref=ins[i].at[target * 2 + 1 - core],
                dst_ref=theirs[i].at[step],
                send_sem=hand_sem.at[i, step],
                recv_sem=take_sem.at[i, step],
                device_id={"dp": partner},
                device_id_type=MESH,
            )
            swap.start()
            swaps[i, step] = swap
    hops = {}
    for step in range(chips):
        for i, way in enumerate(ways):
            rows = ins[i].shape[1]
            tile = min(rows, 16)
            loads[i, step].wait()
            swaps[i, step].wait_recv()
            if step:
                hops[i, step - 1].wait_recv()
            last = step == chips - 1
            into = outs[i] if last else (moving[i].at[step - 1] if step else mine[i].at[step])

            @pl.loop(0, rows // tile)
            def _(block):
                span = pl.ds(pl.multiple_of(block * tile, tile), tile)
                total = mine[i][step, span, :].astype(jnp.float32) + theirs[i][
                    step, span, :
                ].astype(jnp.float32)
                if step:
                    total = total + moving[i][step - 1, span, :].astype(jnp.float32)
                into[span, :] = total.astype(into.dtype)

            if not last:
                hop = pltpu.make_async_remote_copy(
                    src_ref=into,
                    dst_ref=moving[i].at[step],
                    send_sem=send_sem.at[i, step],
                    recv_sem=recv_sem.at[i, step],
                    device_id={"dp": nexts[way]},
                    device_id_type=MESH,
                )
                hop.start()
                hops[i, step] = hop
    for copy in list(hops.values()) + list(swaps.values()):
        copy.wait_send()


def scatter_all(grads, ways, ranks):
    chips, count = ranks // 2, len(grads)
    grads = [g.reshape(ranks, g.shape[0] // ranks, g.shape[1]) for g in grads]
    dma = pltpu.SemaphoreType.DMA
    blocks = [g.shape[1:] for g in grads]
    return pl.pallas_call(
        functools.partial(scatter_kernel, chips, ways),
        out_shape=[jax.ShapeDtypeStruct(b, jnp.float32) for b in blocks],
        in_specs=[pl.BlockSpec(memory_space=pl.ANY)] * count,
        out_specs=[pl.BlockSpec(memory_space=pltpu.VMEM)] * count,
        scratch_shapes=[pltpu.VMEM((chips,) + b, jnp.bfloat16) for b in blocks]
        + [pltpu.VMEM((chips,) + b, jnp.bfloat16) for b in blocks]
        + [pltpu.VMEM((chips - 1,) + b, jnp.bfloat16) for b in blocks]
        + [
            dma((count, chips)),
            dma((count, chips - 1)),
            dma((count, chips - 1)),
            dma((count, chips)),
            dma((count, chips)),
        ],
        compiler_params=pltpu.CompilerParams(
            collective_id=2, has_side_effects=True, vmem_limit_bytes=56 * 1024 * 1024
        ),
    )(*grads)


def both(values):
    other = lax.ppermute(values, "tensor", [(0, 1), (1, 0)])
    return jnp.concatenate([values, other], axis=0)


def halves_sum(terms):
    half = terms.shape[0] // 2
    sent = lax.ppermute(terms[half:].astype(jnp.bfloat16), "tensor", [(0, 1), (1, 0)])
    return terms[:half] + sent.astype(jnp.float32)


def reset_masks(segment):
    same_one = jnp.concatenate([jnp.zeros((1,), jnp.bool_), segment[1:] == segment[:-1]])
    same_two = jnp.concatenate([jnp.zeros((2,), jnp.bool_), segment[2:] == segment[:-2]])
    masks = jnp.stack([same_one, same_two]).astype(jnp.float32)
    half = segment.shape[0] // 2
    turned = jnp.concatenate([masks[:, half:], masks[:, :half]], axis=1)
    masks = jnp.where(lax.axis_index("tensor") == 0, masks, turned)
    return (masks[0][:, None], masks[1][:, None])


def turn(values, offset):
    return jnp.concatenate([values[-offset:], values[:-offset]], axis=0)


def dot(left, right, dims):
    return lax.dot_general(left, right, (dims, ((), ())), preferred_element_type=jnp.float32)


GATHER_WAYS = (1, -1, -1, -1)


def local(
    tokens,
    segment_ids,
    norm1_gain,
    in_proj,
    conv_weight,
    out_proj,
    norm2_gain,
    gate_up,
    down_proj,
    cotangent,
    *,
    ranks,
):
    rows, _, channels = in_proj.shape
    hidden_units = gate_up.shape[2]
    lift_full, in_full, out_full, down_full = gather_all(
        [
            gate_up.reshape(rows, 2 * hidden_units),
            in_proj.reshape(rows, 3 * channels),
            out_proj,
            down_proj,
        ],
        GATHER_WAYS,
        ranks,
    )
    offset = lax.axis_index("tensor") * channels
    kernel = lax.dynamic_slice_in_dim(conv_weight, offset, channels, 1)
    mask_one, mask_two = reset_masks(segment_ids[0])
    inputs = tokens.astype(jnp.float32)
    normed_one, factor_one = rms_forward(inputs, norm1_gain)
    rows_one = both(normed_one.astype(jnp.bfloat16))
    cot_rows = both(cotangent)
    projected = dot(rows_one, in_full, ((1,), (0,)))
    b_part = projected[:, :channels]
    c_part = projected[:, channels : 2 * channels]
    x_part = projected[:, 2 * channels :]
    mixed_in = b_part * x_part
    mixed_one = mask_one * turn(mixed_in, 1)
    mixed_two = mask_two * turn(mixed_in, 2)
    conv_out = kernel[0] * mixed_in + kernel[1] * mixed_one + kernel[2] * mixed_two
    gated = (c_part * conv_out).astype(jnp.bfloat16)
    resid = inputs + halves_sum(dot(gated, out_full, ((1,), (1,))))
    normed_two, factor_two = rms_forward(resid, norm2_gain)
    rows_two = both(normed_two.astype(jnp.bfloat16))
    lifted = dot(rows_two, lift_full, ((1,), (0,)))
    gate_lin, up_lin = lifted[:, :hidden_units], lifted[:, hidden_units:]
    sigmoid_gate = jax.nn.sigmoid(gate_lin)
    activ = gate_lin * sigmoid_gate
    hidden = (activ * up_lin).astype(jnp.bfloat16)
    block_out = resid + halves_sum(dot(hidden, down_full, ((1,), (1,))))
    grad_down = dot(cot_rows, hidden, ((0,), (0,))).astype(jnp.bfloat16)
    back_hidden = dot(cot_rows, down_full, ((1,), (0,)))
    back_gate = (
        back_hidden * up_lin * sigmoid_gate * (1.0 + gate_lin * (1.0 - sigmoid_gate))
    ).astype(jnp.bfloat16)
    back_up = (back_hidden * activ).astype(jnp.bfloat16)
    back_lifted = jnp.concatenate([back_gate, back_up], axis=1)
    grad_lift = dot(rows_two, back_lifted, ((0,), (0,))).astype(jnp.bfloat16)
    back_normed2 = halves_sum(dot(back_lifted, lift_full, ((1,), (1,))))
    resid_part, gain_two = rms_backward(resid, factor_two, norm2_gain, back_normed2)
    back_resid = cotangent.astype(jnp.float32) + resid_part
    resid_rows = both(back_resid.astype(jnp.bfloat16))
    grad_out = dot(resid_rows, gated, ((0,), (0,))).astype(jnp.bfloat16)
    back_gated = dot(resid_rows, out_full, ((1,), (0,)))
    back_c = back_gated * conv_out
    back_conv = back_gated * c_part
    back_mixed = (
        kernel[0] * back_conv
        + turn(kernel[1] * mask_one * back_conv, -1)
        + turn(kernel[2] * mask_two * back_conv, -2)
    )
    conv_local = jnp.stack(
        [
            jnp.sum(back_conv * mixed_in, axis=0),
            jnp.sum(back_conv * mixed_one, axis=0),
            jnp.sum(back_conv * mixed_two, axis=0),
        ]
    )
    back_proj = jnp.concatenate(
        [back_mixed * x_part, back_c, back_mixed * b_part], axis=1
    ).astype(jnp.bfloat16)
    grad_in = dot(rows_one, back_proj, ((0,), (0,))).astype(jnp.bfloat16)
    back_normed1 = halves_sum(dot(back_proj, in_full, ((1,), (1,))))
    input_part, gain_one = rms_backward(inputs, factor_one, norm1_gain, back_normed1)
    grad_tokens = back_resid + input_part
    conv_placed = lax.dynamic_update_slice_in_dim(
        jnp.zeros(conv_weight.shape, jnp.float32), conv_local, offset, 1
    )
    small = jnp.concatenate([gain_one[None], gain_two[None], conv_placed], axis=0)
    small = lax.psum(small, ("dp", "tensor"))
    lift_shard, in_shard, out_shard, down_shard = scatter_all(
        [grad_lift, grad_in, grad_out, grad_down], GATHER_WAYS, ranks
    )
    return (
        block_out,
        grad_tokens,
        small[0],
        in_shard.reshape(in_proj.shape),
        small[2:],
        out_shard,
        small[1],
        lift_shard.reshape(gate_up.shape),
        down_shard,
    )


def solution(mesh):
    placed = (
        P(("dp", "tensor"), None),
        P("dp", None),
        P(),
        P("dp", None, "tensor"),
        P(),
        P("dp", "tensor"),
        P(),
        P("dp", None, "tensor"),
        P("dp", "tensor"),
        P(("dp", "tensor"), None),
    )
    return jax.shard_map(
        functools.partial(local, ranks=mesh.shape["dp"]),
        mesh=mesh,
        in_specs=placed,
        out_specs=(
            P(("dp", "tensor"), None),
            P(("dp", "tensor"), None),
            P(),
            P("dp", None, "tensor"),
            P(),
            P("dp", "tensor"),
            P(),
            P("dp", None, "tensor"),
            P("dp", "tensor"),
        ),
        check_vma=False,
    )
```

time: 819 us -> 325 us (0.40)
  waiting for transfers between devices: 634 us -> 23 us
  Pallas kernels: 0 us -> 202 us
  blocking collectives: 81.1 us -> 40 us
  matrix products: 51.5 us -> 27.7 us
  between operations: 14.4 us -> 1.05 us
  starting transfers between devices: 0.67 us -> 9 us
    reduce_scatter x7 -> x0, waiting for transfers between devices: 330 us -> none  [the longest x1 142 us: local(): lax.psum_scatter(grad_lift, 'dp', scatter_dimension=0, tiled=True)]
    pallas_call x0 -> x2, Pallas kernels: none -> 202 us  [the longest x1 102 us: scatter_all(): pl.pallas_call(functools.partial(scatter_kernel, chips, ways), out_shape=...]
    all_gather x4 -> x0, waiting for transfers between devices: 187 us -> none  [the longest x1 72.5 us: local(): lax.all_gather(gate_up, 'dp', axis=0, tiled=True)]
    unnamed x13 -> x0, waiting for transfers between devices: 117 us -> none
    all_gather x4 -> x0, blocking collectives: 40.9 us -> none  [the longest x1 13.6 us: local(): cot_rows = lax.all_gather(cotangent, 'tensor', axis=0, tiled=True)]
    dot_general x12, matrix products: 51.5 us -> 27.7 us  [dot(): lax.dot_general(left, right, (dims, ((), ())), preferred_element_type=jnp...]
    ppermute x0 -> x8, waiting for transfers between devices: none -> 23 us  [the longest x4 12.3 us: both(): other = lax.ppermute(values, 'tensor', [(0, 1), (1, 0)])]
    unnamed x53 -> x40, local copies, waits for them, and re-layouts: 20.5 us -> 5.76 us
  transfers between devices with their start and end apart: 12 -> 8, of which waited for: 11 -> 5; matrix products, arithmetic and copies ran while one was open for 8% -> 8% of each run, Pallas kernels for 0% -> 62%
where the time goes in v1:
time: 325 us
  Pallas kernels  202 us (62%)
  blocking collectives  40 us (12%)
  matrix products  27.7 us (9%)
  waiting for transfers between devices  23 us (7%)
  local copies, waits for them, and re-layouts  13.7 us (4%)
  starting transfers between devices  9 us (3%)
  other arithmetic  7.75 us (2%)
    pallas_call x1, Pallas kernels, scatter_all(): pl.pallas_call(functools.partial(scatter_kernel, chips, ways), out_shape=...  102 us
    pallas_call x1, Pallas kernels, gather_all(): pl.pallas_call(functools.partial(gather_kernel, chips, ways), out_shape=[...  101 us
    psum x1, blocking collectives, local(): small = lax.psum(small, ('dp', 'tensor'))  40 us
    dot_general x12, matrix products, dot(): lax.dot_general(left, right, (dims, ((), ())), preferred_element_type=jnp...  27.7 us
    ppermute x4, waiting for transfers between devices, both(): other = lax.ppermute(values, 'tensor', [(0, 1), (1, 0)])  12.3 us
    ppermute x4, waiting for transfers between devices, halves_sum(): lax.ppermute(terms[half:].astype(jnp.bfloat16), 'tensor', [(0, 1), (1, 0)])  10.6 us
  transfers between devices with their start and end apart: 8, of which 5 were waited for; matrix products, arithmetic and copies ran while one was open for 8% of the time, Pallas kernels for 62%

profile of v1, /device:TPU:0, one launch (start us, length us, event | category | flops | bytes accessed | tf_op | source)
XLA Modules:
  0.0 324.7 jit_solution(13180000622846225057)
XLA Ops:
  0.6 1.1 fusion.2
  1.7 1.1 fusion.4
  2.8 0.0 copy-start.9
  2.8 3.0 collective-permute-start
  5.9 0.8 compare_reduce_fusion.1
  6.7 0.8 compare_reduce_fusion
  7.6 0.1 pad_add_fusion
  7.7 0.1 concatenate.45
  7.8 0.9 constant_dynamic-slice_fusion
  8.7 1.9 copy.25
  10.6 1.6 copy.24
  12.2 100.7 %shard_map.169 = (bf16[16,64,4608]{2,1,0:T(8,128)(2,1)}, bf16[16,64,1536]{2,1,0:T(8,128)(2,1)}, bf16[16,64,512]{2,1,0:T(8,128)(2,1)}, bf16[16,64,2304]{2,1,0:T(8,128)(2,1)}) custom-call(bf16[64,4608]{1,0:T(8,128)(2,1)} %bitcast.57, bf16[64,1536]{1,0:T(8,128)(2,1)} %bitcast.59, bf16[64,512]{1,0:T(8,128)(2,1)} %refs_2_.1, bf16[64,2304]{1,0:T(8,128)(2,1)} %refs_3_.1), custom_call_target="tpu_custom_call" | custom-call | tf_op jit(solution)/shard_map/pallas_call | solution.py:106
  113.0 0.0 collective-permute-done
  113.0 2.9 fusion.15
  115.9 0.0 copy-start.8
  115.9 0.1 slice_multiply_fusion
  116.0 0.0 copy-start.1
  116.0 0.0 copy-start.14
  116.0 0.3 multiply_convert_fusion.7
  116.4 0.7 copy-done.2
  117.1 0.5 fusion.30
  117.6 0.6 collective-permute-start.1
  118.2 1.5 collective-permute-start.4
  119.7 7.1 %collective-permute-done.1 = bf16[128,1024]{1,0:T(8,128)(2,1)S(1)} collective-permute-done((bf16[128,1024]{1,0:T(8,128)(2,1)S(1)}, bf16[128,1024]{1,0:T(8,128)(2,1)S(1)}, u32[]{:S(2)}, u32[]{:S(2)}) %collective-permute-start.1) | collective-permute-done | bytes 262176 | tf_op jit(solution)/shard_map/ppermute | solution.py:223
  126.9 0.2 multiply_reduce_fusion.5
  127.1 0.1 multiply_convert_fusion.6
  127.2 0.6 collective-permute-start.2
  127.8 4.7 %collective-permute-done.4 = bf16[128,1024]{1,0:T(8,128)(2,1)S(1)} collective-permute-done((bf16[128,1024]{1,0:T(8,128)(2,1)S(1)}, bf16[128,1024]{1,0:T(8,128)(2,1)S(1)}, u32[]{:S(2)}, u32[]{:S(2)}) %collective-permute-start.4) | collective-permute-done | bytes 262176 | tf_op jit(solution)/shard_map/ppermute | solution.py:217
  132.5 5.0 %collective-permute-done.2 = bf16[128,1024]{1,0:T(8,128)(2,1)S(1)} collective-permute-done((bf16[128,1024]{1,0:T(8,128)(2,1)S(1)}, bf16[128,1024]{1,0:T(8,128)(2,1)S(1)}, u32[]{:S(2)}, u32[]{:S(2)}) %collective-permute-start.2) | collective-permute-done | bytes 262176 | tf_op jit(solution)/shard_map/ppermute | solution.py:217
  137.5 2.6 fusion.14
  140.1 3.3 %multiply_convert_fusion.1 = (bf16[256,2304]{1,0:T(8,128)(2,1)}, bf16[256,2304]{1,0:T(8,128)(2,1)}, bf16[256,2304]{1,0:T(8,128)(2,1)S(1)}) fusion(f32[256,4608]{1,0:T(8,128)S(1)} %fusion.14, bf16[256,1024]{1,0:T(8,128)(2,1)S(1)} %constant_dynamic-update-slice_fusion, bf16[1024,2304]{1,0:T(8,128)(2,1)S(1)} %bitcast.85), kind=kOutput, calls=%fused_computation.5 | convolution fusion | flops 1216806912 | bytes 13500416 | tf_op jit(solution)/shard_map/dot_general | solution.py:242
  143.4 1.4 fusion.31
  144.9 0.6 collective-permute-start.3
  145.5 2.6 fusion.1
  148.2 1.6 collective-permute-start.5
  149.7 5.1 %convolution_convert_fusion = bf16[1024,4608]{1,0:T(8,128)(2,1)} fusion(bf16[256,2304]{1,0:T(8,128)(2,1)S(1)} %copy-done.7, bf16[256,2304]{1,0:T(8,128)(2,1)S(1)} %copy-done.6, bf16[128,1024]{1,0:T(8,128)(2,1)S(1)} %collective-permute-done.2, bf16[128,1024]{1,0:T(8,128)(2,1)S(1)} %multiply_convert_fusion.6), kind=kOutput, calls=%fused_computation | convolution fusion | flops 2426404864 | bytes 12320768 | tf_op jit(solution)/shard_map/dot_general | solution.py:242
  154.8 3.5 %collective-permute-done.5 = bf16[128,1024]{1,0:T(8,128)(2,1)S(1)} collective-permute-done((bf16[128,1024]{1,0:T(8,128)(2,1)S(1)}, bf16[128,1024]{1,0:T(8,128)(2,1)S(1)}, u32[]{:S(2)}, u32[]{:S(2)}) %collective-permute-start.5) | collective-permute-done | bytes 262176 | tf_op jit(solution)/shard_map/ppermute | solution.py:223
  158.3 0.2 multiply_reduce_fusion.3
  158.5 0.0 collective-permute-done.3
  158.5 1.1 fusion.26
  159.6 0.5 collective-permute-start.6
  160.1 3.7 %convolution_convert_fusion.1 = bf16[1024,2304]{1,0:T(8,128)(2,1)} fusion(bf16[256,1024]{1,0:T(8,128)(2,1)S(1)} %constant_dynamic-update-slice_fusion, bf16[256,2304]{1,0:T(8,128)(2,1)S(1)} %copy-done.5), kind=kOutput, calls=%fused_computation.1 | convolution fusion | flops 1210318848 | bytes 6422528 | tf_op jit(solution)/shard_map/dot_general | solution.py:242
  163.8 2.7 collective-permute-done.6
  166.5 0.6 multiply_reduce_fusion.2
  167.1 0.2 multiply_multiply_fusion.1
  167.4 0.3 multiply_convert_fusion.5
  167.7 0.1 multiply_convert_fusion.3
  167.8 1.5 copy-done.3
  169.3 1.0 fusion.16
  170.3 0.0 copy-start.10
  170.3 0.6 collective-permute-start.7
  170.9 1.4 convolution_convert_fusion.3
  172.4 2.6 convolution_convert_fusion.2
  175.0 101.7 %shard_map.170 = (f32[64,4608]{1,0:T(8,128)}, f32[64,1536]{1,0:T(8,128)}, f32[64,512]{1,0:T(8,128)}, f32[64,2304]{1,0:T(8,128)}) custom-call(bf16[16,64,4608]{2,1,0:T(8,128)(2,1)} %bitcast.44, bf16[16,64,1536]{2,1,0:T(8,128)(2,1)} %bitcast.54, bf16[16,64,512]{2,1,0:T(8,128)(2,1)} %bitcast.58, bf16[16,64,2304]{2,1,0:T(8,128)(2,1)} %bitcast.45), custom_call_target="tpu_custom_call" | custom-call | tf_op jit(solution)/shard_map/pallas_call | solution.py:195
  276.7 0.0 copy-start.15
  276.7 3.1 reshape.111
  279.9 0.8 copy.27
  280.7 0.2 fusion.10
  280.9 40.0 %psum.7 = f32[5,1024]{1,0:T(8,128)S(1)} all-reduce(f32[5,1024]{1,0:T(8,128)S(1)} %pad_maximum_fusion.15), channel_id=1, replica_groups=mesh['dp'=16,'tensor'=2] {'dp','tensor'}, use_global_device_ids=true, to_apply=%region_9.10 | all-reduce | flops 5120 | bytes 40960 | tf_op jit(solution)/shard_map/psum | solution.py:338
  320.9 0.6 slice.177
  321.5 0.6 fusion.27
  322.2 1.0 fusion.7
  323.2 0.7 copy.32
  323.8 0.8 copy.33
  (55 shorter events, 0.4 us)
Async XLA Ops:
  2.8 113.0 %copy-start.9 = (bf16[128,1024]{1,0:T(8,128)(2,1)}, bf16[128,1024]{1,0:T(8,128)(2,1)S(1)}, u32[]{:S(2)}) copy-start(bf16[128,1024]{1,0:T(8,128)(2,1)S(1)} %fusion.4) | copy-start | bytes 786436
  2.8 110.1 %collective-permute-start = (bf16[128,1024]{1,0:T(8,128)(2,1)S(1)}, bf16[128,1024]{1,0:T(8,128)(2,1)S(1)}, u32[]{:S(2)}, u32[]{:S(2)}) collective-permute-start(bf16[128,1024]{1,0:T(8,128)(2,1)S(1)} %fusion.4), channel_id=1, source_target_pairs={{0,1},{1,0},{2,3},{3,2},{4,5},{5,4},{6,7},{7,6},{8,9},{9,8},{10,11... | collective-permute-start | bytes 786440 | tf_op jit(solution)/shard_map/ppermute | solution.py:217
  115.9 1.2 copy-start.2
  115.9 2.3 copy-start.8
  116.0 10.8 %copy-start.1 = (bf16[128,1024]{1,0:T(8,128)(2,1)S(1)}, bf16[128,1024]{1,0:T(8,128)(2,1)}, u32[]{:S(2)}) copy-start(bf16[128,1024]{1,0:T(8,128)(2,1)} %param.10) | copy-start | bytes 786436
  116.0 11.0 %copy-start.14 = (f32[1024]{0:T(1024)S(1)}, f32[1024]{0:T(1024)}, u32[]{:S(2)}) copy-start(f32[1024]{0:T(1024)} %param.16) | copy-start | bytes 12292
  116.0 21.5 %copy-start = (bf16[16,64,4608]{2,1,0:T(8,128)(2,1)S(1)}, bf16[16,64,4608]{2,1,0:T(8,128)(2,1)}, u32[]{:S(2)}) copy-start(bf16[16,64,4608]{2,1,0:T(8,128)(2,1)} %get-tuple-element.19) | copy-start | bytes 28311556
  117.6 9.2 %collective-permute-start.1 = (bf16[128,1024]{1,0:T(8,128)(2,1)S(1)}, bf16[128,1024]{1,0:T(8,128)(2,1)S(1)}, u32[]{:S(2)}, u32[]{:S(2)}) collective-permute-start(bf16[128,1024]{1,0:T(8,128)(2,1)S(1)} %slice.224), channel_id=1, source_target_pairs={{0,1},{1,0},{2,3},{3,2},{4,5},{5,4},{6,7},{7,6},{8,9},{9,8},{10,11... | collective-permute-start | bytes 786440 | tf_op jit(solution)/shard_map/ppermute | solution.py:223
  118.2 14.3 %collective-permute-start.4 = (bf16[128,1024]{1,0:T(8,128)(2,1)S(1)}, bf16[128,1024]{1,0:T(8,128)(2,1)S(1)}, u32[]{:S(2)}, u32[]{:S(2)}) collective-permute-start(bf16[128,1024]{1,0:T(8,128)(2,1)S(1)} %copy-done.8), channel_id=1, source_target_pairs={{0,1},{1,0},{2,3},{3,2},{4,5},{5,4},{6,7},{7,6},{8,9},{9,8},{10,11... | collective-permute-start | bytes 786440 | tf_op jit(solution)/shard_map/ppermute | solution.py:217
  127.2 10.3 %collective-permute-start.2 = (bf16[128,1024]{1,0:T(8,128)(2,1)S(1)}, bf16[128,1024]{1,0:T(8,128)(2,1)S(1)}, u32[]{:S(2)}, u32[]{:S(2)}) collective-permute-start(bf16[128,1024]{1,0:T(8,128)(2,1)S(1)} %multiply_convert_fusion.6), channel_id=1, source_target_pairs={{0,1},{1,0},{2,3},{3,2},{4,5},{5,4},{6,7},{7,6},{8,9},{9,8},{10,11... | collective-permute-start | bytes 786440 | tf_op jit(solution)/shard_map/ppermute | solution.py:217
  132.5 7.6 %slice-start = ((s8[4718592]{0:T(1024)(128)(4,1)}), s8[4194304]{0:T(1024)(128)(4,1)S(1)}, s32[]{:S(2)}) async-start(s8[4718592]{0:T(1024)(128)(4,1)} %bitcast.83), calls=%async_computation | async-start | bytes 8388608
  137.5 2.6 slice-start.1
  143.4 1.4 copy-start.4
  143.4 2.1 copy-start.6
  143.4 2.1 copy-start.7
  144.9 13.6 %collective-permute-start.3 = (bf16[128,1024]{1,0:T(8,128)(2,1)S(1)}, bf16[128,1024]{1,0:T(8,128)(2,1)S(1)}, u32[]{:S(2)}, u32[]{:S(2)}) collective-permute-start(bf16[128,1024]{1,0:T(8,128)(2,1)S(1)} %slice.223), channel_id=1, source_target_pairs={{0,1},{1,0},{2,3},{3,2},{4,5},{5,4},{6,7},{7,6},{8,9},{9,8},{10,11... | collective-permute-start | bytes 786440 | tf_op jit(solution)/shard_map/ppermute | solution.py:223
  148.2 10.1 %collective-permute-start.5 = (bf16[128,1024]{1,0:T(8,128)(2,1)S(1)}, bf16[128,1024]{1,0:T(8,128)(2,1)S(1)}, u32[]{:S(2)}, u32[]{:S(2)}) collective-permute-start(bf16[128,1024]{1,0:T(8,128)(2,1)S(1)} %slice.222), channel_id=1, source_target_pairs={{0,1},{1,0},{2,3},{3,2},{4,5},{5,4},{6,7},{7,6},{8,9},{9,8},{10,11... | collective-permute-start | bytes 786440 | tf_op jit(solution)/shard_map/ppermute | solution.py:223
  154.8 5.3 %copy-start.5 = (bf16[256,2304]{1,0:T(8,128)(2,1)S(1)}, bf16[256,2304]{1,0:T(8,128)(2,1)}, u32[]{:S(2)}) copy-start(bf16[256,2304]{1,0:T(8,128)(2,1)} %copy-done.4) | copy-start | bytes 3538948
  159.6 6.9 %collective-permute-start.6 = (bf16[128,1024]{1,0:T(8,128)(2,1)S(1)}, bf16[128,1024]{1,0:T(8,128)(2,1)S(1)}, u32[]{:S(2)}, u32[]{:S(2)}) collective-permute-start(bf16[128,1024]{1,0:T(8,128)(2,1)S(1)} %get-tuple-element.53), channel_id=1, source_target_pairs={{0,1},{1,0},{2,3},{3,2},{4,5},{5,4},{6,7},{7,6},{8,9},{9,8},{10,11... | collective-permute-start | bytes 786440 | tf_op jit(solution)/shard_map/ppermute | solution.py:217
  167.4 1.9 copy-start.3
  170.3 2.1 copy-start.10
  170.3 110.3 %collective-permute-start.7 = (bf16[128,1024]{1,0:T(8,128)(2,1)S(1)}, bf16[128,1024]{1,0:T(8,128)(2,1)S(1)}, u32[]{:S(2)}, u32[]{:S(2)}) collective-permute-start(bf16[128,1024]{1,0:T(8,128)(2,1)S(1)} %slice.221), channel_id=1, source_target_pairs={{0,1},{1,0},{2,3},{3,2},{4,5},{5,4},{6,7},{7,6},{8,9},{9,8},{10,11... | collective-permute-start | bytes 786440 | tf_op jit(solution)/shard_map/ppermute | solution.py:223
  276.7 3.1 copy-start.12
  276.7 3.9 %copy-start.15 = (f32[1024]{0:T(1024)S(1)}, f32[1024]{0:T(1024)}, u32[]{:S(2)}) copy-start(f32[1024]{0:T(1024)} %param.12) | copy-start | bytes 12292
  279.8 43.3 %copy-start.13 = (f32[64,512]{1,0:T(8,128)S(1)}, f32[64,512]{1,0:T(8,128)}, u32[]{:S(2)}) copy-start(f32[64,512]{1,0:T(8,128)} %get-tuple-element.93) | copy-start | bytes 393220
  279.8 44.0 %copy-start.11 = (f32[64,2304]{1,0:T(8,128)S(1)}, f32[64,2304]{1,0:T(8,128)}, u32[]{:S(2)}) copy-start(f32[64,2304]{1,0:T(8,128)} %get-tuple-element.96) | copy-start | bytes 1769476

commit v2 on v1

--- a/solution.py
+++ b/solution.py
@@ -45,20 +45,41 @@
 
 def greet(others):
     barrier = pltpu.get_barrier_semaphore()
+    peer = 1 - lax.axis_index("tensor")
+    pl.semaphore_signal(barrier, inc=1, device_id={"tensor": peer}, device_id_type=MESH)
     for other in others:
         pl.semaphore_signal(barrier, inc=1, device_id={"dp": other}, device_id_type=MESH)
-    pl.semaphore_wait(barrier, len(others))
+    pl.semaphore_wait(barrier, len(others) + 1)
+
+
+def across(source, into, send_sem, recv_sem):
+    return pltpu.make_async_remote_copy(
+        src_ref=source,
+        dst_ref=into,
+        send_sem=send_sem,
+        recv_sem=recv_sem,
+        device_id={"tensor": 1 - lax.axis_index("tensor")},
+        device_id_type=MESH,
+    )
 
 
 def gather_kernel(chips, ways, *refs):
     count = len(ways)
-    ins, outs = refs[:count], refs[count : 2 * count]
-    own_sem, send_sem, recv_sem, hand_sem, take_sem = refs[2 * count :]
+    pairs = (len(refs) - 2 * count - 7) // 2
+    swaps_in, refs = refs[:pairs], refs[pairs:]
+    ins, refs = refs[:count], refs[count:]
+    swaps_out, refs = refs[:pairs], refs[pairs:]
+    outs = refs[:count]
+    own_sem, send_sem, recv_sem, hand_sem, take_sem, out_sem, in_sem = refs[count:]
     me, core, chip, owner = ring_place(chips)
     partner = chip * 2 + 1 - core
     nexts = {way: owner(way) * 2 + core for way in (1, -1)}
     greet((nexts[1], nexts[-1], partner))
     own, started = [], []
+    for i in range(pairs):
+        swap = across(swaps_in[i], swaps_out[i], out_sem.at[i], in_sem.at[i])
+        swap.start()
+        started.append((swap, True))
     arriving = [None] * count
     for step in range(chips):
         for i, way in enumerate(ways):
@@ -100,37 +121,52 @@
         keep.wait()
 
 
-def gather_all(shards, ways, ranks):
-    chips, count = ranks // 2, len(shards)
+def gather_all(swapped, shards, ways, ranks):
+    chips, count, pairs = ranks // 2, len(shards), len(swapped)
     dma = pltpu.SemaphoreType.DMA
-    gathered = pl.pallas_call(
+    outs = pl.pallas_call(
         functools.partial(gather_kernel, chips, ways),
-        out_shape=[jax.ShapeDtypeStruct((ranks,) + s.shape, s.dtype) for s in shards],
-        in_specs=[pl.BlockSpec(memory_space=pltpu.VMEM)] * count,
-        out_specs=[pl.BlockSpec(memory_space=pl.ANY)] * count,
+        out_shape=[jax.ShapeDtypeStruct(s.shape, s.dtype) for s in swapped]
+        + [jax.ShapeDtypeStruct((ranks,) + s.shape, s.dtype) for s in shards],
+        in_specs=[pl.BlockSpec(memory_space=pltpu.VMEM)] * (pairs + count),
+        out_specs=[pl.BlockSpec(memory_space=pltpu.VMEM)] * pairs
+        + [pl.BlockSpec(memory_space=pl.ANY)] * count,
         scratch_shapes=[
             dma((count,)),
             dma((count, chips - 1)),
             dma((count, chips - 1)),
             dma((count, chips)),
             dma((count, chips)),
+            dma((pairs,)),
+            dma((pairs,)),
         ],
         compiler_params=pltpu.CompilerParams(collective_id=1, has_side_effects=True),
-    )(*shards)
-    return [g.reshape(ranks * s.shape[0], s.shape[1]) for g, s in zip(gathered, shards)]
+    )(*swapped, *shards)
+    full = [g.reshape(ranks * s.shape[0], s.shape[1]) for g, s in zip(outs[pairs:], shards)]
+    return outs[:pairs], full
 
 
 def scatter_kernel(chips, ways, *refs):
     count = len(ways)
-    ins, outs = refs[:count], refs[count : 2 * count]
-    mine = refs[2 * count : 3 * count]
-    theirs = refs[3 * count : 4 * count]
-    moving = refs[4 * count : 5 * count]
-    load_sem, send_sem, recv_sem, hand_sem, take_sem = refs[5 * count :]
+    small_in, row_in, refs = refs[0], refs[1], refs[2:]
+    ins, refs = refs[:count], refs[count:]
+    small_out, row_out, refs = refs[0], refs[1], refs[2:]
+    outs, refs = refs[:count], refs[count:]
+    mine = refs[:count]
+    theirs = refs[count : 2 * count]
+    moving = refs[2 * count : 3 * count]
+    smalls, folded, folded_other, refs = *refs[3 * count : 3 * count + 3], refs[3 * count + 3 :]
+    load_sem, send_sem, recv_sem, hand_sem, take_sem, own_sem, out_sem, in_sem = refs[:8]
+    small_send, small_recv, small_hand, small_take = refs[8:]
     me, core, chip, owner = ring_place(chips)
     partner = chip * 2 + 1 - core
     nexts = {way: owner(way) * 2 + core for way in (1, -1)}
     greet((nexts[1], nexts[-1], partner))
+    row_swap = across(row_in, row_out, out_sem.at[0], in_sem.at[0])
+    row_swap.start()
+    keep = pltpu.make_async_copy(small_in, smalls.at[me], own_sem)
+    keep.start()
+    small_hops, small_hands = [], []
     loads, swaps = {}, {}
     for step in range(chips):
         for i, way in enumerate(ways):
@@ -152,6 +188,40 @@
             swaps[i, step] = swap
     hops = {}
     for step in range(chips):
+        slot = owner(-step) * 2 + core
+        if step:
+            small_hops[step - 1].wait_recv()
+        source = smalls.at[slot] if step else small_in
+        if step < chips - 1:
+            ring = pltpu.make_async_remote_copy(
+                src_ref=source,
+                dst_ref=smalls.at[slot],
+                send_sem=small_send.at[step],
+                recv_sem=small_recv.at[step],
+                device_id={"dp": nexts[1]},
+                device_id_type=MESH,
+            )
+            ring.start()
+            small_hops.append(ring)
+        hand = pltpu.make_async_remote_copy(
+            src_ref=source,
+            dst_ref=smalls.at[slot],
+            send_sem=small_hand.at[step],
+            recv_sem=small_take.at[step],
+            device_id={"dp": partner},
+            device_id_type=MESH,
+        )
+        hand.start()
+        small_hands.append(hand)
+        if step == chips - 1:
+            keep.wait()
+            for hand in small_hands:
+                hand.wait_recv()
+            folded[...] = lax.fori_loop(
+                1, 2 * chips, lambda k, total: total + smalls[k], smalls[0]
+            )
+            fold_swap = across(folded, folded_other, out_sem.at[1], in_sem.at[1])
+            fold_swap.start()
         for i, way in enumerate(ways):
             rows = ins[i].shape[1]
             tile = min(rows, 16)
@@ -183,34 +253,48 @@
                 )
                 hop.start()
                 hops[i, step] = hop
-    for copy in list(hops.values()) + list(swaps.values()):
+    fold_swap.wait()
+    small_out[...] = folded[...] + folded_other[...]
+    row_swap.wait()
+    for copy in list(hops.values()) + list(swaps.values()) + small_hops + small_hands:
         copy.wait_send()
 
 
-def scatter_all(grads, ways, ranks):
+def scatter_all(small, rows, grads, ways, ranks):
     chips, count = ranks // 2, len(grads)
     grads = [g.reshape(ranks, g.shape[0] // ranks, g.shape[1]) for g in grads]
     dma = pltpu.SemaphoreType.DMA
     blocks = [g.shape[1:] for g in grads]
     return pl.pallas_call(
         functools.partial(scatter_kernel, chips, ways),
-        out_shape=[jax.ShapeDtypeStruct(b, jnp.float32) for b in blocks],
-        in_specs=[pl.BlockSpec(memory_space=pl.ANY)] * count,
-        out_specs=[pl.BlockSpec(memory_space=pltpu.VMEM)] * count,
+        out_shape=[jax.ShapeDtypeStruct(v.shape, v.dtype) for v in (small, rows)]
+        + [jax.ShapeDtypeStruct(b, jnp.float32) for b in blocks],
+        in_specs=[pl.BlockSpec(memory_space=pltpu.VMEM)] * 2
+        + [pl.BlockSpec(memory_space=pl.ANY)] * count,
+        out_specs=[pl.BlockSpec(memory_space=pltpu.VMEM)] * (count + 2),
         scratch_shapes=[pltpu.VMEM((chips,) + b, jnp.bfloat16) for b in blocks]
         + [pltpu.VMEM((chips,) + b, jnp.bfloat16) for b in blocks]
         + [pltpu.VMEM((chips - 1,) + b, jnp.bfloat16) for b in blocks]
+        + [pltpu.VMEM((ranks,) + small.shape, small.dtype)]
+        + [pltpu.VMEM(small.shape, small.dtype)] * 2
         + [
             dma((count, chips)),
             dma((count, chips - 1)),
             dma((count, chips - 1)),
             dma((count, chips)),
             dma((count, chips)),
+            dma,
+            dma((2,)),
+            dma((2,)),
+            dma((chips - 1,)),
+            dma((chips - 1,)),
+            dma((chips,)),
+            dma((chips,)),
         ],
         compiler_params=pltpu.CompilerParams(
             collective_id=2, has_side_effects=True, vmem_limit_bytes=56 * 1024 * 1024
         ),
-    )(*grads)
+    )(small, rows, *grads)
 
 
 def both(values):
@@ -242,7 +326,7 @@
     return lax.dot_general(left, right, (dims, ((), ())), preferred_element_type=jnp.float32)
 
 
-GATHER_WAYS = (1, -1, -1, -1)
+WAYS = (-1, -1, 1, 1, -1)
 
 
 def local(
@@ -260,24 +344,26 @@
     ranks,
 ):
     rows, _, channels = in_proj.shape
-    hidden_units = gate_up.shape[2]
-    lift_full, in_full, out_full, down_full = gather_all(
+    inputs = tokens.astype(jnp.float32)
+    normed_one, factor_one = rms_forward(inputs, norm1_gain)
+    normed_one = normed_one.astype(jnp.bfloat16)
+    (normed_other, cot_other), (in_full, out_full, gate_full, up_full, down_full) = gather_all(
+        [normed_one, cotangent],
         [
-            gate_up.reshape(rows, 2 * hidden_units),
             in_proj.reshape(rows, 3 * channels),
             out_proj,
+            gate_up[:, 0, :],
+            gate_up[:, 1, :],
             down_proj,
         ],
-        GATHER_WAYS,
+        WAYS,
         ranks,
     )
+    rows_one = jnp.concatenate([normed_one, normed_other], axis=0)
+    cot_rows = jnp.concatenate([cotangent, cot_other], axis=0)
     offset = lax.axis_index("tensor") * channels
     kernel = lax.dynamic_slice_in_dim(conv_weight, offset, channels, 1)
     mask_one, mask_two = reset_masks(segment_ids[0])
-    inputs = tokens.astype(jnp.float32)
-    normed_one, factor_one = rms_forward(inputs, norm1_gain)
-    rows_one = both(normed_one.astype(jnp.bfloat16))
-    cot_rows = both(cotangent)
     projected = dot(rows_one, in_full, ((1,), (0,)))
     b_part = projected[:, :channels]
     c_part = projected[:, channels : 2 * channels]
@@ -290,21 +376,23 @@
     resid = inputs + halves_sum(dot(gated, out_full, ((1,), (1,))))
     normed_two, factor_two = rms_forward(resid, norm2_gain)
     rows_two = both(normed_two.astype(jnp.bfloat16))
-    lifted = dot(rows_two, lift_full, ((1,), (0,)))
-    gate_lin, up_lin = lifted[:, :hidden_units], lifted[:, hidden_units:]
+    gate_lin = dot(rows_two, gate_full, ((1,), (0,)))
+    up_lin = dot(rows_two, up_full, ((1,), (0,)))
     sigmoid_gate = jax.nn.sigmoid(gate_lin)
     activ = gate_lin * sigmoid_gate
     hidden = (activ * up_lin).astype(jnp.bfloat16)
-    block_out = resid + halves_sum(dot(hidden, down_full, ((1,), (1,))))
+    ffn_terms = dot(hidden, down_full, ((1,), (1,)))
     grad_down = dot(cot_rows, hidden, ((0,), (0,))).astype(jnp.bfloat16)
     back_hidden = dot(cot_rows, down_full, ((1,), (0,)))
     back_gate = (
         back_hidden * up_lin * sigmoid_gate * (1.0 + gate_lin * (1.0 - sigmoid_gate))
     ).astype(jnp.bfloat16)
     back_up = (back_hidden * activ).astype(jnp.bfloat16)
-    back_lifted = jnp.concatenate([back_gate, back_up], axis=1)
-    grad_lift = dot(rows_two, back_lifted, ((0,), (0,))).astype(jnp.bfloat16)
-    back_normed2 = halves_sum(dot(back_lifted, lift_full, ((1,), (1,))))
+    grad_gate = dot(rows_two, back_gate, ((0,), (0,))).astype(jnp.bfloat16)
+    grad_up = dot(rows_two, back_up, ((0,), (0,))).astype(jnp.bfloat16)
+    back_normed2 = halves_sum(
+        dot(back_gate, gate_full, ((1,), (1,))) + dot(back_up, up_full, ((1,), (1,)))
+    )
     resid_part, gain_two = rms_backward(resid, factor_two, norm2_gain, back_normed2)
     back_resid = cotangent.astype(jnp.float32) + resid_part
     resid_rows = both(back_resid.astype(jnp.bfloat16))
@@ -334,20 +422,27 @@
     conv_placed = lax.dynamic_update_slice_in_dim(
         jnp.zeros(conv_weight.shape, jnp.float32), conv_local, offset, 1
     )
-    small = jnp.concatenate([gain_one[None], gain_two[None], conv_placed], axis=0)
-    small = lax.psum(small, ("dp", "tensor"))
-    lift_shard, in_shard, out_shard, down_shard = scatter_all(
-        [grad_lift, grad_in, grad_out, grad_down], GATHER_WAYS, ranks
-    )
+    small = jnp.concatenate(
+        [gain_one[None], gain_two[None], conv_placed, jnp.zeros_like(conv_placed)], axis=0
+    )
+    half = ffn_terms.shape[0] // 2
+    small, ffn_other, in_shard, out_shard, gate_shard, up_shard, down_shard = scatter_all(
+        small,
+        ffn_terms[half:].astype(jnp.bfloat16),
+        [grad_in, grad_out, grad_gate, grad_up, grad_down],
+        WAYS,
+        ranks,
+    )
+    block_out = resid + (ffn_terms[:half] + ffn_other.astype(jnp.float32))
     return (
         block_out,
         grad_tokens,
         small[0],
         in_shard.reshape(in_proj.shape),
-        small[2:],
+        small[2:5],
         out_shard,
         small[1],
-        lift_shard.reshape(gate_up.shape),
+        jnp.stack([gate_shard, up_shard], axis=1),
         down_shard,
     )
 

time: 325 us -> 284 us (0.87)
  blocking collectives: 40 us -> 0 us
  waiting for transfers between devices: 23 us -> 17.6 us
    psum x1 -> x0, blocking collectives: 40 us -> none  [local(): small = lax.psum(small, ('dp', 'tensor'))]
    ppermute x4 -> x2, waiting for transfers between devices: 12.3 us -> 6.09 us  [both(): other = lax.ppermute(values, 'tensor', [(0, 1), (1, 0)])]
    slice x1 -> x3, local copies, waits for them, and re-layouts: 0.61 us -> 4.44 us  [the longest x1 2.33 us: local(): gate_up[:, 1, :]]
    dot_general x12 -> x15, matrix products: 27.7 us -> 29.2 us  [dot(): lax.dot_general(left, right, (dims, ((), ())), preferred_element_type=jnp...]
    ppermute x4 -> x3, waiting for transfers between devices: 10.6 us -> 11.5 us  [halves_sum(): lax.ppermute(terms[half:].astype(jnp.bfloat16), 'tensor', [(0, 1), (1, 0)])]
  transfers between devices with their start and end apart: 8 -> 5, of which waited for: 5 -> 5; matrix products, arithmetic and copies ran while one was open for 8% -> 4% of each run, Pallas kernels for 62% -> 0%
where the time goes in v2:
time: 284 us
  Pallas kernels  202 us (71%)
  matrix products  29.2 us (10%)
  waiting for transfers between devices  17.6 us (6%)
  local copies, waits for them, and re-layouts  16.4 us (6%)
  other arithmetic  9.28 us (3%)
  starting transfers between devices  7.79 us (3%)
    pallas_call x1, Pallas kernels, scatter_all(): pl.pallas_call(functools.partial(scatter_kernel, chips, ways), out_shape=...  103 us
    pallas_call x1, Pallas kernels, gather_all(): pl.pallas_call(functools.partial(gather_kernel, chips, ways), out_shape=[...  99.2 us
    dot_general x15, matrix products, dot(): lax.dot_general(left, right, (dims, ((), ())), preferred_element_type=jnp...  29.2 us
    ppermute x3, waiting for transfers between devices, halves_sum(): lax.ppermute(terms[half:].astype(jnp.bfloat16), 'tensor', [(0, 1), (1, 0)])  11.5 us
    ppermute x2, waiting for transfers between devices, both(): other = lax.ppermute(values, 'tensor', [(0, 1), (1, 0)])  6.09 us
  transfers between devices with their start and end apart: 5, of which 5 were waited for; matrix products, arithmetic and copies ran while one was open for 4% of the time, Pallas kernels for 0%

profile of v2, /device:TPU:0, one launch (start us, length us, event | category | flops | bytes accessed | tf_op | source)
XLA Modules:
  0.0 283.6 jit_solution(9485765573778616160)
XLA Ops:
  0.6 0.0 copy-start
  0.7 0.8 compare_reduce_fusion
  1.5 0.8 compare_reduce_fusion.1
  2.4 1.1 fusion.1
  3.5 1.6 copy.32
  5.1 2.3 fusion.24
  7.4 0.8 fusion.3.refs_0_
  8.3 0.9 copy_bitcast_fusion.1
  9.1 99.2 %shard_map.169 = (bf16[128,1024]{1,0:T(8,128)(2,1)}, bf16[128,1024]{1,0:T(8,128)(2,1)}, bf16[16,64,1536]{2,1,0:T(8,128)(2,1)}, bf16[16,64,512]{2,1,0:T(8,128)(2,...) custom-call(bf16[128,1024]{1,0:T(8,128)(2,1)} %fusion.3.refs_0_, ...), custom_call_target="tpu_custom_call" | custom-call | tf_op jit(solution)/shard_map/pallas_call | solution.py:127
  108.3 3.0 %fusion.13 = f32[256,1536]{1,0:T(8,128)S(1)} fusion(bf16[1024,1536]{1,0:T(8,128)(2,1)} %bitcast.66, bf16[128,1024]{1,0:T(8,128)(2,1)} %get-tuple-element.23, bf16[128,1024]{1,0:T(8,128)(2,1)S(1)} %copy-done.3), kind=kOutput, calls=%fused_computation.63 | convolution fusion | flops 806354944 | bytes 5242880 | tf_op jit(solution)/shard_map/dot_general | solution.py:326
  111.3 0.1 slice_multiply_fusion
  111.4 0.1 concatenate.42
  111.5 0.1 pad_add_fusion
  111.7 0.9 constant_dynamic-slice_fusion
  112.5 0.3 multiply_convert_fusion.7
  112.9 0.0 copy-start.14
  112.9 0.5 fusion.28
  113.4 1.6 collective-permute-start
  115.0 7.0 %collective-permute-done = bf16[128,1024]{1,0:T(8,128)(2,1)S(1)} collective-permute-done((bf16[128,1024]{1,0:T(8,128)(2,1)S(1)}, bf16[128,1024]{1,0:T(8,128)(2,1)S(1)}, u32[]{:S(2)}, u32[]{:S(2)}) %collective-permute-start) | collective-permute-done | bytes 262176 | tf_op jit(solution)/shard_map/ppermute | solution.py:307
  122.0 0.2 multiply_reduce_fusion.5
  122.2 0.0 slice-start
  122.3 0.0 slice-start.2
  122.3 0.1 multiply_convert_fusion.6
  122.4 1.6 collective-permute-start.1
  124.0 1.4 fusion.30
  125.3 4.8 %collective-permute-done.1 = bf16[128,1024]{1,0:T(8,128)(2,1)S(1)} collective-permute-done((bf16[128,1024]{1,0:T(8,128)(2,1)S(1)}, bf16[128,1024]{1,0:T(8,128)(2,1)S(1)}, u32[]{:S(2)}, u32[]{:S(2)}) %collective-permute-start.1) | collective-permute-done | bytes 262176 | tf_op jit(solution)/shard_map/ppermute | solution.py:301
  130.2 1.4 fusion.20
  131.6 2.1 multiply_convert_fusion
  133.7 1.4 fusion.29
  135.1 0.0 copy-start.6
  135.1 3.7 %convolution_convert_fusion = bf16[1024,2304]{1,0:T(8,128)(2,1)} fusion(bf16[256,1024]{1,0:T(8,128)(2,1)S(1)} %constant_dynamic-update-slice_fusion, bf16[256,2304]{1,0:T(8,128)(2,1)S(1)} %get-tuple-element.74), kind=kOutput, calls=%fused_computation | convolution fusion | flops 1210318848 | bytes 6422528 | tf_op jit(solution)/shard_map/dot_general | solution.py:326
  138.8 1.6 fusion.31
  140.4 1.4 convolution_add_fusion
  141.9 1.6 collective-permute-start.2
  143.4 0.7 slice.208.refs_1_
  144.2 3.6 %convolution_convert_fusion.2 = bf16[1024,2304]{1,0:T(8,128)(2,1)} fusion(bf16[256,2304]{1,0:T(8,128)(2,1)S(1)} %get-tuple-element.73, bf16[128,1024]{1,0:T(8,128)(2,1)S(1)} %collective-permute-done.1, bf16[128,1024]{1,0:T(8,128)(2,1)S(1)} %multiply_convert_fusion.6), kind=kOutput, calls=%fused_computation.2 | convolution fusion | flops 1211367424 | bytes 6422528 | tf_op jit(solution)/shard_map/dot_general | solution.py:326
  147.8 1.1 collective-permute-done.2
  148.8 0.2 multiply_reduce_fusion.3
  149.0 0.2 fusion.23
  149.2 1.6 collective-permute-start.3
  150.8 3.6 %convolution_convert_fusion.1 = bf16[1024,2304]{1,0:T(8,128)(2,1)} fusion(bf16[256,2304]{1,0:T(8,128)(2,1)S(1)} %get-tuple-element.72, bf16[128,1024]{1,0:T(8,128)(2,1)S(1)} %collective-permute-done.1, bf16[128,1024]{1,0:T(8,128)(2,1)S(1)} %multiply_convert_fusion.6), kind=kOutput, calls=%fused_computation.1 | convolution fusion | flops 1211367424 | bytes 6422528 | tf_op jit(solution)/shard_map/dot_general | solution.py:326
  154.4 1.3 collective-permute-done.3
  155.7 0.5 multiply_multiply_fusion
  156.2 0.3 multiply_reduce_fusion.2
  156.6 0.3 multiply_convert_fusion.5
  156.8 0.1 multiply_convert_fusion.3
  156.9 1.5 copy-done.2
  158.5 1.0 fusion.14
  159.5 2.6 convolution_convert_fusion.3
  162.2 1.6 collective-permute-start.4
  163.8 1.5 convolution_convert_fusion.4
  165.2 3.4 %collective-permute-done.4 = bf16[128,1024]{1,0:T(8,128)(2,1)S(1)} collective-permute-done((bf16[128,1024]{1,0:T(8,128)(2,1)S(1)}, bf16[128,1024]{1,0:T(8,128)(2,1)S(1)}, u32[]{:S(2)}, u32[]{:S(2)}) %collective-permute-start.4) | collective-permute-done | bytes 262176 | tf_op jit(solution)/shard_map/ppermute | solution.py:307
  168.6 0.2 fusion.9
  168.8 0.6 pad_maximum_fusion.11.refs_0_
  169.5 103.1 %shard_map.170 = (f32[8,1024]{1,0:T(8,128)}, bf16[128,1024]{1,0:T(8,128)(2,1)}, f32[64,1536]{1,0:T(8,128)}, f32[64,512]{1,0:T(8,128)}, f32[64,2304]{1,0:T(8,128)...) custom-call(f32[8,1024]{1,0:T(8,128)} %pad_maximum_fusion.11.refs_0_, bf16[128,1024]{1,0:T(8,128)(2,1)} %slice.208.refs_1_, ...), custom_call_target="tpu_custom_call" | custom-call | tf_op jit(solution)/shard_map/pallas_call | solution.py:268
  272.6 1.5 fusion.25
  274.1 1.4 slice.149
  275.4 1.8 fusion.10
  277.3 1.8 copy.36
  279.1 0.1 pad_maximum_fusion
  279.2 1.9 copy.28
  281.1 1.0 fusion.8
  282.1 0.7 copy.41
  282.8 0.8 copy.42
  (62 shorter events, 0.4 us)
Async XLA Ops:
  0.6 6.8 %copy-start = (bf16[128,1024]{1,0:T(8,128)(2,1)S(1)}, bf16[128,1024]{1,0:T(8,128)(2,1)}, u32[]{:S(2)}) copy-start(bf16[128,1024]{1,0:T(8,128)(2,1)} %param.10) | copy-start | bytes 786436
  0.7 6.8 %copy-start.15 = (f32[1024]{0:T(1024)S(1)}, f32[1024]{0:T(1024)}, u32[]{:S(2)}) copy-start(f32[1024]{0:T(1024)} %param.12) | copy-start | bytes 12292
  8.3 100.1 %copy-start.3 = (bf16[128,1024]{1,0:T(8,128)(2,1)S(1)}, bf16[128,1024]{1,0:T(8,128)(2,1)}, u32[]{:S(2)}) copy-start(bf16[128,1024]{1,0:T(8,128)(2,1)} %fusion.3.refs_0_) | copy-start | bytes 786436
  111.3 1.6 copy-start.1
  112.5 2.4 copy-start.5
  112.8 2.1 copy-start.12
  112.9 9.4 %copy-start.14 = (f32[1024]{0:T(1024)S(1)}, f32[1024]{0:T(1024)}, u32[]{:S(2)}) copy-start(f32[1024]{0:T(1024)} %param.16) | copy-start | bytes 12292
  112.9 11.1 %copy-start.16 = (bf16[16,64,2304]{2,1,0:T(8,128)(2,1)S(1)}, bf16[16,64,2304]{2,1,0:T(8,128)(2,1)}, u32[]{:S(2)}) copy-start(bf16[16,64,2304]{2,1,0:T(8,128)(2,1)} %get-tuple-element.28) | copy-start | bytes 14155780
  113.4 8.6 %collective-permute-start = (bf16[128,1024]{1,0:T(8,128)(2,1)S(1)}, bf16[128,1024]{1,0:T(8,128)(2,1)S(1)}, u32[]{:S(2)}, u32[]{:S(2)}) collective-permute-start(bf16[128,1024]{1,0:T(8,128)(2,1)S(1)} %slice.211), channel_id=1, source_target_pairs={{0,1},{1,0},{2,3},{3,2},{4,5},{5,4},{6,7},{7,6},{8,9},{9,8},{10,11... | collective-permute-start | bytes 786440 | tf_op jit(solution)/shard_map/ppermute | solution.py:307
  122.2 7.9 %slice-start = ((s8[4718592]{0:T(1024)(128)(4,1)}), s8[4194304]{0:T(1024)(128)(4,1)S(1)}, s32[]{:S(2)}) async-start(s8[4718592]{0:T(1024)(128)(4,1)} %bitcast.93), calls=%async_computation | async-start | bytes 8388608
  122.3 9.3 %slice-start.2 = ((s8[4718592]{0:T(1024)(128)(4,1)}), s8[4194304]{0:T(1024)(128)(4,1)S(1)}, s32[]{:S(2)}) async-start(s8[4718592]{0:T(1024)(128)(4,1)} %bitcast.97), calls=%async_computation.2 | async-start | bytes 8388608
  122.4 7.8 %collective-permute-start.1 = (bf16[128,1024]{1,0:T(8,128)(2,1)S(1)}, bf16[128,1024]{1,0:T(8,128)(2,1)S(1)}, u32[]{:S(2)}, u32[]{:S(2)}) collective-permute-start(bf16[128,1024]{1,0:T(8,128)(2,1)S(1)} %multiply_convert_fusion.6), channel_id=1, source_target_pairs={{0,1},{1,0},{2,3},{3,2},{4,5},{5,4},{6,7},{7,6},{8,9},{9,8},{10,11... | collective-permute-start | bytes 786440 | tf_op jit(solution)/shard_map/ppermute | solution.py:301
  123.9 6.2 %slice-start.1 = ((s8[4718592]{0:T(1024)(128)(4,1)}), s8[524288]{0:T(1024)(128)(4,1)S(1)}, s32[]{:S(2)}) async-start(s8[4718592]{0:T(1024)(128)(4,1)} %bitcast.93), calls=%async_computation.1 | async-start | bytes 1048576
  123.9 7.6 %slice-start.3 = ((s8[4718592]{0:T(1024)(128)(4,1)}), s8[524288]{0:T(1024)(128)(4,1)S(1)}, s32[]{:S(2)}) async-start(s8[4718592]{0:T(1024)(128)(4,1)} %bitcast.97), calls=%async_computation.3 | async-start | bytes 1048576
  135.1 8.3 %copy-start.6 = (f32[256,1024]{1,0:T(8,128)}, f32[256,1024]{1,0:T(8,128)S(1)}, u32[]{:S(2)}) copy-start(f32[256,1024]{1,0:T(8,128)S(1)} %fusion.29) | copy-start | bytes 3145732
  141.9 6.9 %collective-permute-start.2 = (bf16[128,1024]{1,0:T(8,128)(2,1)S(1)}, bf16[128,1024]{1,0:T(8,128)(2,1)S(1)}, u32[]{:S(2)}, u32[]{:S(2)}) collective-permute-start(bf16[128,1024]{1,0:T(8,128)(2,1)S(1)} %slice.210), channel_id=1, source_target_pairs={{0,1},{1,0},{2,3},{3,2},{4,5},{5,4},{6,7},{7,6},{8,9},{9,8},{10,11... | collective-permute-start | bytes 786440 | tf_op jit(solution)/shard_map/ppermute | solution.py:307
  149.2 6.4 %collective-permute-start.3 = (bf16[128,1024]{1,0:T(8,128)(2,1)S(1)}, bf16[128,1024]{1,0:T(8,128)(2,1)S(1)}, u32[]{:S(2)}, u32[]{:S(2)}) collective-permute-start(bf16[128,1024]{1,0:T(8,128)(2,1)S(1)} %get-tuple-element.66), channel_id=1, source_target_pairs={{0,1},{1,0},{2,3},{3,2},{4,5},{5,4},{6,7},{7,6},{8,9},{9,8},{10,11... | collective-permute-start | bytes 786440 | tf_op jit(solution)/shard_map/ppermute | solution.py:301
  156.6 1.9 copy-start.2
  158.5 1.0 copy-start.4
  158.5 1.0 copy-start.11
  162.2 6.4 %collective-permute-start.4 = (bf16[128,1024]{1,0:T(8,128)(2,1)S(1)}, bf16[128,1024]{1,0:T(8,128)(2,1)S(1)}, u32[]{:S(2)}, u32[]{:S(2)}) collective-permute-start(bf16[128,1024]{1,0:T(8,128)(2,1)S(1)} %slice.209), channel_id=1, source_target_pairs={{0,1},{1,0},{2,3},{3,2},{4,5},{5,4},{6,7},{7,6},{8,9},{9,8},{10,11... | collective-permute-start | bytes 786440 | tf_op jit(solution)/shard_map/ppermute | solution.py:307
  169.5 106.0 %copy-start.7 = (f32[256,1024]{1,0:T(8,128)S(1)}, f32[256,1024]{1,0:T(8,128)}, u32[]{:S(2)}) copy-start(f32[256,1024]{1,0:T(8,128)} %copy-done.6) | copy-start | bytes 3145732
  272.6 6.5 %copy-start.9 = (f32[64,2304]{1,0:T(8,128)S(1)}, f32[64,2304]{1,0:T(8,128)}, u32[]{:S(2)}) copy-start(f32[64,2304]{1,0:T(8,128)} %get-tuple-element.34) | copy-start | bytes 1769476
  272.6 6.5 %copy-start.10 = (f32[64,2304]{1,0:T(8,128)S(1)}, f32[64,2304]{1,0:T(8,128)}, u32[]{:S(2)}) copy-start(f32[64,2304]{1,0:T(8,128)} %get-tuple-element.35) | copy-start | bytes 1769476
  279.2 3.0 %copy-start.13 = (f32[64,512]{1,0:T(8,128)S(1)}, f32[64,512]{1,0:T(8,128)}, u32[]{:S(2)}) copy-start(f32[64,512]{1,0:T(8,128)} %get-tuple-element.108) | copy-start | bytes 393220
  279.2 3.6 %copy-start.8 = (f32[64,2304]{1,0:T(8,128)S(1)}, f32[64,2304]{1,0:T(8,128)}, u32[]{:S(2)}) copy-start(f32[64,2304]{1,0:T(8,128)} %get-tuple-element.111) | copy-start | bytes 1769476

commit v3 on v2

--- a/solution.py
+++ b/solution.py
@@ -24,6 +24,9 @@
 
 
 MESH = pl.DeviceIdType.MESH
+
+WAYS = (-1, -1, 1, 1, -1)
+BACKWARD = (1, 0, 1, 0, 0)
 
 
 def chip_at(pos, chips):
@@ -80,14 +83,14 @@
         swap = across(swaps_in[i], swaps_out[i], out_sem.at[i], in_sem.at[i])
         swap.start()
         started.append((swap, True))
-    arriving = [None] * count
+    arriving, direct = [None] * count, {}
     for step in range(chips):
         for i, way in enumerate(ways):
             slot = owner(-way * step) * 2 + core
             if step:
                 arriving[i].wait_recv()
             source = outs[i].at[slot] if step else ins[i]
-            if step < chips - 1:
+            if step < chips - 1 and not (BACKWARD[i] and step == chips - 2):
                 ring = pltpu.make_async_remote_copy(
                     src_ref=source,
                     dst_ref=outs[i].at[slot],
@@ -99,6 +102,19 @@
                 ring.start()
                 arriving[i] = ring
                 started.append((ring, False))
+            if BACKWARD[i] and step == chips - 2:
+                arriving[i] = direct[i]
+            if BACKWARD[i] and step == 0:
+                direct[i] = pltpu.make_async_remote_copy(
+                    src_ref=source,
+                    dst_ref=outs[i].at[slot],
+                    send_sem=send_sem.at[i, chips - 2],
+                    recv_sem=recv_sem.at[i, chips - 2],
+                    device_id={"dp": nexts[-way]},
+                    device_id_type=MESH,
+                )
+                direct[i].start()
+                started.append((direct[i], False))
             hand = pltpu.make_async_remote_copy(
                 src_ref=source,
                 dst_ref=outs[i].at[slot],
@@ -227,10 +243,13 @@
             tile = min(rows, 16)
             loads[i, step].wait()
             swaps[i, step].wait_recv()
-            if step:
-                hops[i, step - 1].wait_recv()
             last = step == chips - 1
-            into = outs[i] if last else (moving[i].at[step - 1] if step else mine[i].at[step])
+            added = [step - 1] if step > BACKWARD[i] else []
+            if last and BACKWARD[i]:
+                added.append(0)
+            for hop in added:
+                hops[i, hop].wait_recv()
+            into = outs[i] if last else (moving[i].at[step - 1] if added else mine[i].at[step])
 
             @pl.loop(0, rows // tile)
             def _(block):
@@ -238,8 +257,8 @@
                 total = mine[i][step, span, :].astype(jnp.float32) + theirs[i][
                     step, span, :
                 ].astype(jnp.float32)
-                if step:
-                    total = total + moving[i][step - 1, span, :].astype(jnp.float32)
+                for hop in added:
+                    total = total + moving[i][hop, span, :].astype(jnp.float32)
                 into[span, :] = total.astype(into.dtype)
 
             if not last:
@@ -248,7 +267,7 @@
                     dst_ref=moving[i].at[step],
                     send_sem=send_sem.at[i, step],
                     recv_sem=recv_sem.at[i, step],
-                    device_id={"dp": nexts[way]},
+                    device_id={"dp": nexts[-way if BACKWARD[i] and step == 0 else way]},
                     device_id_type=MESH,
                 )
                 hop.start()
@@ -309,8 +328,8 @@
 
 
 def reset_masks(segment):
-    same_one = jnp.concatenate([jnp.zeros((1,), jnp.bool_), segment[1:] == segment[:-1]])
-    same_two = jnp.concatenate([jnp.zeros((2,), jnp.bool_), segment[2:] == segment[:-2]])
+    padded = jnp.concatenate([jnp.full((2,), -1, segment.dtype), segment])
+    same_one, same_two = segment == padded[1:-1], segment == padded[:-2]
     masks = jnp.stack([same_one, same_two]).astype(jnp.float32)
     half = segment.shape[0] // 2
     turned = jnp.concatenate([masks[:, half:], masks[:, :half]], axis=1)
@@ -324,9 +343,6 @@
 
 def dot(left, right, dims):
     return lax.dot_general(left, right, (dims, ((), ())), preferred_element_type=jnp.float32)
-
-
-WAYS = (-1, -1, 1, 1, -1)
 
 
 def local(

time: 284 us -> 280 us (0.986)
  no operation moved by 1% of the time
where the time goes in v3:
time: 280 us; the launch traced here: 279 us
  Pallas kernels  200 us (71%)
  matrix products  29.1 us (10%)
  waiting for transfers between devices  17.6 us (6%)
  local copies, waits for them, and re-layouts  16.3 us (6%)
  starting transfers between devices  7.79 us (3%)
  other arithmetic  7.64 us (3%)
    pallas_call x1, Pallas kernels, scatter_all(): pl.pallas_call(functools.partial(scatter_kernel, chips, ways), out_shape=...  101 us
    pallas_call x1, Pallas kernels, gather_all(): pl.pallas_call(functools.partial(gather_kernel, chips, ways), out_shape=[...  98.8 us
    dot_general x15, matrix products, dot(): lax.dot_general(left, right, (dims, ((), ())), preferred_element_type=jnp...  29.1 us
    ppermute x3, waiting for transfers between devices, halves_sum(): lax.ppermute(terms[half:].astype(jnp.bfloat16), 'tensor', [(0, 1), (1, 0)])  11.5 us
    ppermute x2, waiting for transfers between devices, both(): other = lax.ppermute(values, 'tensor', [(0, 1), (1, 0)])  6.1 us
  transfers between devices with their start and end apart: 5, of which 5 were waited for; matrix products, arithmetic and copies ran while one was open for 4% of the time, Pallas kernels for 0%

profile of v3, /device:TPU:0, one launch (start us, length us, event | category | flops | bytes accessed | tf_op | source)
XLA Modules:
  0.0 279.4 jit_solution(1548013588298196619)
XLA Ops:
  0.7 1.1 fusion.1
  1.8 1.6 copy.32
  3.4 2.3 fusion.26
  5.8 0.8 fusion.3.refs_0_
  6.6 0.9 copy_bitcast_fusion.1
  7.5 98.8 %shard_map.169 = (bf16[128,1024]{1,0:T(8,128)(2,1)}, bf16[128,1024]{1,0:T(8,128)(2,1)}, bf16[16,64,1536]{2,1,0:T(8,128)(2,1)}, bf16[16,64,512]{2,1,0:T(8,128)(2,...) custom-call(bf16[128,1024]{1,0:T(8,128)(2,1)} %fusion.3.refs_0_, ...), custom_call_target="tpu_custom_call" | custom-call | tf_op jit(solution)/shard_map/pallas_call | solution.py:143
  106.3 0.0 copy-start.16
  106.3 3.0 %fusion.13 = f32[256,1536]{1,0:T(8,128)S(1)} fusion(bf16[1024,1536]{1,0:T(8,128)(2,1)} %bitcast.67, bf16[128,1024]{1,0:T(8,128)(2,1)} %get-tuple-element.23, bf16[128,1024]{1,0:T(8,128)(2,1)S(1)} %copy-done.3), kind=kOutput, calls=%fused_computation.63 | convolution fusion | flops 806354944 | bytes 5242880 | tf_op jit(solution)/shard_map/dot_general | solution.py:345
  109.3 0.1 slice_multiply_fusion
  109.4 0.1 fusion.15
  109.6 0.9 constant_dynamic-slice_fusion
  110.5 0.3 multiply_convert_fusion.7
  110.8 0.0 copy-start.14
  110.8 0.5 fusion.30
  111.3 1.6 collective-permute-start
  112.9 7.0 %collective-permute-done = bf16[128,1024]{1,0:T(8,128)(2,1)S(1)} collective-permute-done((bf16[128,1024]{1,0:T(8,128)(2,1)S(1)}, bf16[128,1024]{1,0:T(8,128)(2,1)S(1)}, u32[]{:S(2)}, u32[]{:S(2)}) %collective-permute-start) | collective-permute-done | bytes 262176 | tf_op jit(solution)/shard_map/ppermute | solution.py:326
  120.0 0.2 multiply_reduce_fusion.5
  120.1 0.0 copy-done.14
  120.2 0.0 slice-start
  120.2 0.0 slice-start.2
  120.2 0.1 multiply_convert_fusion.6
  120.3 1.6 collective-permute-start.1
  121.9 1.4 fusion.32
  123.2 4.8 %collective-permute-done.1 = bf16[128,1024]{1,0:T(8,128)(2,1)S(1)} collective-permute-done((bf16[128,1024]{1,0:T(8,128)(2,1)S(1)}, bf16[128,1024]{1,0:T(8,128)(2,1)S(1)}, u32[]{:S(2)}, u32[]{:S(2)}) %collective-permute-start.1) | collective-permute-done | bytes 262176 | tf_op jit(solution)/shard_map/ppermute | solution.py:320
  128.1 0.0 slice-done.1
  128.1 1.4 fusion.22
  129.5 0.0 slice-done.2
  129.5 2.1 multiply_convert_fusion
  131.6 1.4 fusion.31
  133.0 0.0 copy-start.6
  133.0 3.7 %convolution_convert_fusion = bf16[1024,2304]{1,0:T(8,128)(2,1)} fusion(bf16[256,1024]{1,0:T(8,128)(2,1)S(1)} %constant_dynamic-update-slice_fusion, bf16[256,2304]{1,0:T(8,128)(2,1)S(1)} %get-tuple-element.74), kind=kOutput, calls=%fused_computation | convolution fusion | flops 1210318848 | bytes 6422528 | tf_op jit(solution)/shard_map/dot_general | solution.py:345
  136.7 1.6 fusion.33
  138.3 1.4 convolution_add_fusion
  139.7 1.6 collective-permute-start.2
  141.3 0.7 slice.198.refs_1_
  142.0 3.6 %convolution_convert_fusion.2 = bf16[1024,2304]{1,0:T(8,128)(2,1)} fusion(bf16[256,2304]{1,0:T(8,128)(2,1)S(1)} %get-tuple-element.73, bf16[128,1024]{1,0:T(8,128)(2,1)S(1)} %collective-permute-done.1, bf16[128,1024]{1,0:T(8,128)(2,1)S(1)} %multiply_convert_fusion.6), kind=kOutput, calls=%fused_computation.2 | convolution fusion | flops 1211367424 | bytes 6422528 | tf_op jit(solution)/shard_map/dot_general | solution.py:345
  145.6 1.1 collective-permute-done.2
  146.7 0.2 multiply_reduce_fusion.3
  146.9 0.2 fusion.25
  147.1 1.6 collective-permute-start.3
  148.6 3.6 %convolution_convert_fusion.1 = bf16[1024,2304]{1,0:T(8,128)(2,1)} fusion(bf16[256,2304]{1,0:T(8,128)(2,1)S(1)} %get-tuple-element.72, bf16[128,1024]{1,0:T(8,128)(2,1)S(1)} %collective-permute-done.1, bf16[128,1024]{1,0:T(8,128)(2,1)S(1)} %multiply_convert_fusion.6), kind=kOutput, calls=%fused_computation.1 | convolution fusion | flops 1211367424 | bytes 6422528 | tf_op jit(solution)/shard_map/dot_general | solution.py:345
  152.3 1.3 collective-permute-done.3
  153.5 0.5 multiply_multiply_fusion
  154.1 0.3 multiply_reduce_fusion.2
  154.4 0.3 multiply_convert_fusion.5
  154.7 0.1 multiply_convert_fusion.3
  154.8 1.5 copy-done.2
  156.3 1.0 fusion.14
  157.4 2.7 convolution_convert_fusion.3
  160.1 1.6 collective-permute-start.4
  161.6 1.5 convolution_convert_fusion.4
  163.1 3.4 %collective-permute-done.4 = bf16[128,1024]{1,0:T(8,128)(2,1)S(1)} collective-permute-done((bf16[128,1024]{1,0:T(8,128)(2,1)S(1)}, bf16[128,1024]{1,0:T(8,128)(2,1)S(1)}, u32[]{:S(2)}, u32[]{:S(2)}) %collective-permute-start.4) | collective-permute-done | bytes 262176 | tf_op jit(solution)/shard_map/ppermute | solution.py:326
  166.5 0.2 fusion.9
  166.7 0.6 pad_maximum_fusion.11.refs_0_
  167.3 101.1 %shard_map.170 = (f32[8,1024]{1,0:T(8,128)}, bf16[128,1024]{1,0:T(8,128)(2,1)}, f32[64,1536]{1,0:T(8,128)}, f32[64,512]{1,0:T(8,128)}, f32[64,2304]{1,0:T(8,128)...) custom-call(f32[8,1024]{1,0:T(8,128)} %pad_maximum_fusion.11.refs_0_, bf16[128,1024]{1,0:T(8,128)(2,1)} %slice.198.refs_1_, ...), custom_call_target="tpu_custom_call" | custom-call | tf_op jit(solution)/shard_map/pallas_call | solution.py:287
  268.4 1.5 fusion.27
  269.9 1.4 slice.137
  271.3 1.8 fusion.10
  273.1 1.8 copy.36
  274.9 0.1 pad_maximum_fusion
  275.0 1.9 copy.28
  276.9 1.0 fusion.8
  278.0 0.7 copy.41
  278.6 0.8 copy.42
  (61 shorter events, 0.4 us)
Async XLA Ops:
  0.6 5.1 %copy-start = (bf16[128,1024]{1,0:T(8,128)(2,1)S(1)}, bf16[128,1024]{1,0:T(8,128)(2,1)}, u32[]{:S(2)}) copy-start(bf16[128,1024]{1,0:T(8,128)(2,1)} %param.10) | copy-start | bytes 786436
  0.7 5.1 %copy-start.15 = (f32[1024]{0:T(1024)S(1)}, f32[1024]{0:T(1024)}, u32[]{:S(2)}) copy-start(f32[1024]{0:T(1024)} %param.12) | copy-start | bytes 12292
  6.6 99.6 %copy-start.3 = (bf16[128,1024]{1,0:T(8,128)(2,1)S(1)}, bf16[128,1024]{1,0:T(8,128)(2,1)}, u32[]{:S(2)}) copy-start(bf16[128,1024]{1,0:T(8,128)(2,1)} %fusion.3.refs_0_) | copy-start | bytes 786436
  106.3 3.1 %copy-start.16 = (s32[1,256]{1,0:T(1,128)S(1)}, s32[1,256]{1,0:T(1,128)}, u32[]{:S(2)}) copy-start(s32[1,256]{1,0:T(1,128)} %param.11) | copy-start | bytes 3076
  109.3 1.5 copy-start.1
  110.5 2.4 copy-start.5
  110.8 2.1 copy-start.12
  110.8 9.4 %copy-start.14 = (f32[1024]{0:T(1024)S(1)}, f32[1024]{0:T(1024)}, u32[]{:S(2)}) copy-start(f32[1024]{0:T(1024)} %param.16) | copy-start | bytes 12292
  110.8 11.1 %copy-start.17 = (bf16[16,64,2304]{2,1,0:T(8,128)(2,1)S(1)}, bf16[16,64,2304]{2,1,0:T(8,128)(2,1)}, u32[]{:S(2)}) copy-start(bf16[16,64,2304]{2,1,0:T(8,128)(2,1)} %get-tuple-element.28) | copy-start | bytes 14155780
  111.3 8.6 %collective-permute-start = (bf16[128,1024]{1,0:T(8,128)(2,1)S(1)}, bf16[128,1024]{1,0:T(8,128)(2,1)S(1)}, u32[]{:S(2)}, u32[]{:S(2)}) collective-permute-start(bf16[128,1024]{1,0:T(8,128)(2,1)S(1)} %slice.201), channel_id=1, source_target_pairs={{0,1},{1,0},{2,3},{3,2},{4,5},{5,4},{6,7},{7,6},{8,9},{9,8},{10,11... | collective-permute-start | bytes 786440 | tf_op jit(solution)/shard_map/ppermute | solution.py:326
  120.2 7.9 %slice-start = ((s8[4718592]{0:T(1024)(128)(4,1)}), s8[4194304]{0:T(1024)(128)(4,1)S(1)}, s32[]{:S(2)}) async-start(s8[4718592]{0:T(1024)(128)(4,1)} %bitcast.95), calls=%async_computation | async-start | bytes 8388608
  120.2 9.3 %slice-start.2 = ((s8[4718592]{0:T(1024)(128)(4,1)}), s8[4194304]{0:T(1024)(128)(4,1)S(1)}, s32[]{:S(2)}) async-start(s8[4718592]{0:T(1024)(128)(4,1)} %bitcast.99), calls=%async_computation.2 | async-start | bytes 8388608
  120.3 7.8 %collective-permute-start.1 = (bf16[128,1024]{1,0:T(8,128)(2,1)S(1)}, bf16[128,1024]{1,0:T(8,128)(2,1)S(1)}, u32[]{:S(2)}, u32[]{:S(2)}) collective-permute-start(bf16[128,1024]{1,0:T(8,128)(2,1)S(1)} %multiply_convert_fusion.6), channel_id=1, source_target_pairs={{0,1},{1,0},{2,3},{3,2},{4,5},{5,4},{6,7},{7,6},{8,9},{9,8},{10,11... | collective-permute-start | bytes 786440 | tf_op jit(solution)/shard_map/ppermute | solution.py:320
  121.9 6.2 %slice-start.1 = ((s8[4718592]{0:T(1024)(128)(4,1)}), s8[524288]{0:T(1024)(128)(4,1)S(1)}, s32[]{:S(2)}) async-start(s8[4718592]{0:T(1024)(128)(4,1)} %bitcast.95), calls=%async_computation.1 | async-start | bytes 1048576
  121.9 7.6 %slice-start.3 = ((s8[4718592]{0:T(1024)(128)(4,1)}), s8[524288]{0:T(1024)(128)(4,1)S(1)}, s32[]{:S(2)}) async-start(s8[4718592]{0:T(1024)(128)(4,1)} %bitcast.99), calls=%async_computation.3 | async-start | bytes 1048576
  133.0 8.3 %copy-start.6 = (f32[256,1024]{1,0:T(8,128)}, f32[256,1024]{1,0:T(8,128)S(1)}, u32[]{:S(2)}) copy-start(f32[256,1024]{1,0:T(8,128)S(1)} %fusion.31) | copy-start | bytes 3145732
  139.7 6.9 %collective-permute-start.2 = (bf16[128,1024]{1,0:T(8,128)(2,1)S(1)}, bf16[128,1024]{1,0:T(8,128)(2,1)S(1)}, u32[]{:S(2)}, u32[]{:S(2)}) collective-permute-start(bf16[128,1024]{1,0:T(8,128)(2,1)S(1)} %slice.200), channel_id=1, source_target_pairs={{0,1},{1,0},{2,3},{3,2},{4,5},{5,4},{6,7},{7,6},{8,9},{9,8},{10,11... | collective-permute-start | bytes 786440 | tf_op jit(solution)/shard_map/ppermute | solution.py:326
  147.1 6.4 %collective-permute-start.3 = (bf16[128,1024]{1,0:T(8,128)(2,1)S(1)}, bf16[128,1024]{1,0:T(8,128)(2,1)S(1)}, u32[]{:S(2)}, u32[]{:S(2)}) collective-permute-start(bf16[128,1024]{1,0:T(8,128)(2,1)S(1)} %get-tuple-element.66), channel_id=1, source_target_pairs={{0,1},{1,0},{2,3},{3,2},{4,5},{5,4},{6,7},{7,6},{8,9},{9,8},{10,11... | collective-permute-start | bytes 786440 | tf_op jit(solution)/shard_map/ppermute | solution.py:320
  154.4 1.9 copy-start.2
  156.3 1.0 copy-start.4
  156.3 1.0 copy-start.11
  160.1 6.4 %collective-permute-start.4 = (bf16[128,1024]{1,0:T(8,128)(2,1)S(1)}, bf16[128,1024]{1,0:T(8,128)(2,1)S(1)}, u32[]{:S(2)}, u32[]{:S(2)}) collective-permute-start(bf16[128,1024]{1,0:T(8,128)(2,1)S(1)} %slice.199), channel_id=1, source_target_pairs={{0,1},{1,0},{2,3},{3,2},{4,5},{5,4},{6,7},{7,6},{8,9},{9,8},{10,11... | collective-permute-start | bytes 786440 | tf_op jit(solution)/shard_map/ppermute | solution.py:326
  167.3 103.9 %copy-start.7 = (f32[256,1024]{1,0:T(8,128)S(1)}, f32[256,1024]{1,0:T(8,128)}, u32[]{:S(2)}) copy-start(f32[256,1024]{1,0:T(8,128)} %copy-done.6) | copy-start | bytes 3145732
  268.4 6.5 %copy-start.9 = (f32[64,2304]{1,0:T(8,128)S(1)}, f32[64,2304]{1,0:T(8,128)}, u32[]{:S(2)}) copy-start(f32[64,2304]{1,0:T(8,128)} %get-tuple-element.34) | copy-start | bytes 1769476
  268.4 6.5 %copy-start.10 = (f32[64,2304]{1,0:T(8,128)S(1)}, f32[64,2304]{1,0:T(8,128)}, u32[]{:S(2)}) copy-start(f32[64,2304]{1,0:T(8,128)} %get-tuple-element.35) | copy-start | bytes 1769476
  275.0 3.0 %copy-start.13 = (f32[64,512]{1,0:T(8,128)S(1)}, f32[64,512]{1,0:T(8,128)}, u32[]{:S(2)}) copy-start(f32[64,512]{1,0:T(8,128)} %get-tuple-element.110) | copy-start | bytes 393220
  275.0 3.6 %copy-start.8 = (f32[64,2304]{1,0:T(8,128)S(1)}, f32[64,2304]{1,0:T(8,128)}, u32[]{:S(2)}) copy-start(f32[64,2304]{1,0:T(8,128)} %get-tuple-element.113) | copy-start | bytes 1769476
